TPU v7x, 32 devices: a whole 2x2x4 slice. The times are simulated.
32 devices in a mesh: group: 2 (over y), row: 4 (over x, core), col: 4 (over z).
Axes of the slice: x: 2, y: 2, z: 4, core: 2. Of those that a mesh axis runs over, the one named last changes fastest.
Arguments:
- patches: bfloat16 [64, 64, 1280], P(('group', 'row'), 'col'), parts along dimension 0, may hold values from -6 to 6
- patch_gain: bfloat16 [1280], replicated, may hold values from 0.25 to 1.75
- patch_bias: bfloat16 [1280], replicated, may hold values from -3 to 3
- merger_up: bfloat16 [5120, 5120], P('col', 'row'), may hold values from -0.078125 to 0.078125
- merger_up_bias: bfloat16 [5120], P('row'), may hold values from -3 to 3
- merger_down: bfloat16 [5120, 8192], P('row', 'col')
- merger_down_bias: bfloat16 [8192], P('col'), may hold values from -1.796875 to 1.796875
- norm_gain: bfloat16 [8192], P('col'), may hold values from 0.25 to 1.75
- w_gate: bfloat16 [8192, 14784], P('col', 'row'), may hold values from -0.0625 to 0.0625
- w_up: bfloat16 [8192, 14784], P('col', 'row'), may hold values from -0.0625 to 0.0625
- hidden_cotangent: bfloat16 [1024, 14784], P(('group', 'col'), 'row'), parts along dimension 0, may hold values from -0.59765625 to 0.59765625
- placement: int32 [64], P('group'), parts along dimension 0, may hold values from 0 to 31, as said below
- patch_counts: int32 [64], P('group'), parts along dimension 0, may hold values from 4 to 64, as said below
Outputs:
- merger_up_grad: float32 [10240, 5120], P(('group', 'col'), 'row'), parts along dimension 0
- merger_up_bias_grad: float32 [10240], P(('group', 'row')), parts along dimension 0
- merger_down_grad: float32 [10240, 8192], P(('group', 'row'), 'col'), parts along dimension 0
- merger_down_bias_grad: float32 [16384], P(('group', 'col')), parts along dimension 0
There are 2 independent parts, one for each index of `group`. A program takes and returns all parts, laid end to end along the dimension named above; an argument that names none is the same for every part. Nothing has to cross between parts.
Inputs may be any that keep to these rules, and one draw needn't show every extreme that they name: `placement`: A permutation of the images onto the sequence blocks. Block b lies on index b // 8 of row, and image i on index i // 8. The 8 images of one index of row fill at most 2 blocks of any one index of row, and exactly 2 for some pair of indices in every draw. Every count is a multiple of 4; image i's first patch_counts[i] // 4 merged slots are real and the others are padding; some image has exactly 64 patches in every draw.
All inputs are finite; a program needn't handle non-finite values.
Results may differ from a plain program's by a relative error of at most 0.034.
Values may be sent and summed in bfloat16 or wider, within the bound.
A program may use at most 192 MiB of HBM per device.

v0:
```python
import math

import jax
import jax.numpy as jnp
from jax import lax
from jax.sharding import PartitionSpec as P

D = 8192
BLK = 16
IMG_ROW = 8
CAP = 2


EPS_PATCH = 1e-06
EPS_NORM = 1e-06
CONTRACT_ROWS = (((0,), (0,)), ((), ()))
CONTRACT_COLS = (((1,), (1,)), ((), ()))


def gelu_slope(inputs):
    cumulative = 0.5 * (1.0 + jax.scipy.special.erf(inputs / math.sqrt(2.0)))
    return cumulative + inputs * jnp.exp(-0.5 * inputs * inputs) / math.sqrt(2.0 * math.pi)


def patch_tokens(patches, patch_gain, patch_bias):
    values = patches.astype(jnp.float32)
    center = values - jnp.mean(values, axis=-1, keepdims=True)
    spread = jnp.mean(center * center, axis=-1, keepdims=True)
    normed = center * lax.rsqrt(spread + EPS_PATCH) * patch_gain.astype(
        jnp.float32
    ) + patch_bias.astype(jnp.float32)
    image_count, patch_slots, patch_width = patches.shape
    return normed.astype(jnp.bfloat16).reshape(image_count, patch_slots // 4, 4 * patch_width)


def swiglu_grads(gate_out, up_out, cotangent, valid_rows):
    gate_f = gate_out.astype(jnp.float32)
    up_f = up_out.astype(jnp.float32)
    masked = jnp.where(valid_rows[:, None], cotangent.astype(jnp.float32), 0.0)
    logistic = jax.nn.sigmoid(gate_f)
    grad_gate = (masked * up_f * logistic * (1.0 + gate_f * (1.0 - logistic))).astype(jnp.bfloat16)
    grad_up = (masked * gate_f * logistic).astype(jnp.bfloat16)
    return (grad_gate, grad_up)


def shards(
    patches,
    patch_gain,
    patch_bias,
    merger_up,
    merger_up_bias,
    merger_down,
    merger_down_bias,
    norm_gain,
    w_gate,
    w_up,
    hidden_cotangent,
    placement,
    patch_counts,
):
    n_row = lax.axis_size("row")
    n_col = lax.axis_size("col")
    row_index = lax.axis_index("row")
    col_index = lax.axis_index("col")
    images = placement.shape[0]
    image_ids = jnp.arange(images, dtype=jnp.int32)
    dest_group = placement // IMG_ROW
    home_group = image_ids // IMG_ROW
    earlier = (
        (home_group[:, None] == home_group[None, :])
        & (dest_group[:, None] == dest_group[None, :])
        & (image_ids[None, :] < image_ids[:, None])
    )
    rank_in_group = jnp.sum(earlier.astype(jnp.int32), axis=1)
    first_image = row_index * IMG_ROW
    dest_local = lax.dynamic_slice_in_dim(dest_group, first_image, IMG_ROW)
    rank_local = lax.dynamic_slice_in_dim(rank_in_group, first_image, IMG_ROW)
    group_ids = jnp.arange(n_row, dtype=jnp.int32)
    cap_ids = jnp.arange(CAP, dtype=jnp.int32)
    outgoing = (
        (dest_local[None, None, :] == group_ids[:, None, None])
        & (rank_local[None, None, :] == cap_ids[None, :, None])
    ).astype(jnp.bfloat16)
    block_ids = first_image + jnp.arange(IMG_ROW, dtype=jnp.int32)
    arrives = (placement[None, :] == block_ids[:, None]).astype(jnp.float32)
    home_hot = (home_group[:, None] == group_ids[None, :]).astype(jnp.float32)
    rank_hot = (rank_in_group[:, None] == cap_ids[None, :]).astype(jnp.float32)
    incoming = jnp.einsum("ji,is,ik->jsk", arrives, home_hot, rank_hot).astype(jnp.bfloat16)
    hit_table = placement[:, None] == image_ids[None, :]
    block_fill = jnp.sum(jnp.where(hit_table, (patch_counts // 4)[:, None], 0), axis=0)
    slot_ids = jnp.arange(BLK, dtype=jnp.int32)
    valid_all = (slot_ids[None, :] < block_fill[:, None]).reshape(-1)
    image_tokens = patch_tokens(patches, patch_gain, patch_bias)
    slot_count = image_tokens.shape[1]
    feat_width = image_tokens.shape[2] // n_col
    by_feature = image_tokens.reshape(IMG_ROW, slot_count, n_col, feat_width)
    sending = jnp.einsum(
        "dkj,jsce->dckse", outgoing, by_feature, preferred_element_type=jnp.float32
    ).astype(jnp.bfloat16)
    sending = sending.reshape(n_row * n_col, CAP, slot_count, feat_width)
    received = lax.all_to_all(sending, ("row", "col"), split_axis=0, concat_axis=0, tiled=True)
    received = received.reshape(n_row, n_col, CAP, slot_count, feat_width)
    merged = jnp.einsum(
        "jrk,rckse->jcse", incoming, received, preferred_element_type=jnp.float32
    ).astype(jnp.bfloat16)
    merged = merged.reshape(IMG_ROW * BLK, feat_width)
    gathered_in = lax.all_gather(merged, "row", axis=0, tiled=True)
    tokens = gathered_in.shape[0]
    rows_col = tokens // n_col
    rows_part = gathered_in
    pre_act = lax.psum_scatter(
        jnp.dot(rows_part, merger_up, preferred_element_type=jnp.float32).astype(jnp.bfloat16),
        "col",
        scatter_dimension=0,
        tiled=True,
    ).astype(jnp.float32) + merger_up_bias.astype(jnp.float32)
    hidden_one = jax.nn.gelu(pre_act, approximate=False).astype(jnp.bfloat16)
    hidden_all = lax.all_gather(hidden_one, "col", axis=0, tiled=True)
    rows_part = hidden_all
    merged_out = lax.optimization_barrier(
        (
            lax.psum_scatter(
                jnp.dot(rows_part, merger_down, preferred_element_type=jnp.float32).astype(
                    jnp.bfloat16
                ),
                "row",
                scatter_dimension=0,
                tiled=True,
            ).astype(jnp.float32)
            + merger_down_bias.astype(jnp.float32)
        ).astype(jnp.bfloat16)
    )
    merged_f = merged_out.astype(jnp.float32)
    square_sums = lax.psum(jnp.sum(merged_f * merged_f, axis=1), "col")
    inv_rms = lax.rsqrt(square_sums / D + EPS_NORM)
    gain = norm_gain.astype(jnp.float32)
    normed = (merged_f * inv_rms[:, None] * gain).astype(jnp.bfloat16)
    normed_all = lax.all_gather(normed, "row", axis=0, tiled=True)
    ffw_local = w_gate.shape[1]
    rows_part = normed_all
    gate_up = lax.psum_scatter(
        jnp.concatenate(
            [
                jnp.dot(rows_part, w_gate, preferred_element_type=jnp.float32),
                jnp.dot(rows_part, w_up, preferred_element_type=jnp.float32),
            ],
            axis=1,
        ).astype(jnp.bfloat16),
        "col",
        scatter_dimension=0,
        tiled=True,
    ).astype(jnp.float32)
    gate_out = gate_up[:, :ffw_local].astype(jnp.bfloat16)
    up_out = gate_up[:, ffw_local:].astype(jnp.bfloat16)
    valid_rows = lax.dynamic_slice_in_dim(valid_all, col_index * rows_col, rows_col)
    grad_gate, grad_up = swiglu_grads(gate_out, up_out, hidden_cotangent, valid_rows)
    grad_gate_all, grad_up_all = (
        lax.all_gather(grad_gate, "col", axis=0, tiled=True),
        lax.all_gather(grad_up, "col", axis=0, tiled=True),
    )
    from_gate = lax.dot_general(
        grad_gate_all, w_gate, CONTRACT_COLS, preferred_element_type=jnp.float32
    )
    grad_normed = lax.psum_scatter(
        (
            from_gate
            + lax.dot_general(grad_up_all, w_up, CONTRACT_COLS, preferred_element_type=jnp.float32)
        ).astype(jnp.bfloat16),
        "row",
        scatter_dimension=0,
        tiled=True,
    ).astype(jnp.float32)
    gained = gain * grad_normed
    inner = lax.psum(jnp.sum(merged_f * gained, axis=1), "col")
    grad_merged = (
        inv_rms[:, None] * gained - merged_f * (inv_rms * inv_rms * inv_rms / D * inner)[:, None]
    ).astype(jnp.bfloat16)
    grad_merged_all = lax.all_gather(grad_merged, "row", axis=0, tiled=True)
    merger_down_grad = lax.dot_general(
        hidden_all, grad_merged_all, CONTRACT_ROWS, preferred_element_type=jnp.float32
    )
    merger_down_bias_grad = jnp.sum(grad_merged_all, axis=0, dtype=jnp.float32)
    rows_part = grad_merged_all
    grad_hidden = lax.psum_scatter(
        lax.dot_general(
            rows_part, merger_down, CONTRACT_COLS, preferred_element_type=jnp.float32
        ).astype(jnp.bfloat16),
        "col",
        scatter_dimension=0,
        tiled=True,
    ).astype(jnp.float32)
    grad_pre = (grad_hidden * gelu_slope(pre_act)).astype(jnp.bfloat16)
    grad_pre_all = lax.all_gather(grad_pre, "col", axis=0, tiled=True)
    merger_up_grad = lax.dot_general(
        gathered_in, grad_pre_all, CONTRACT_ROWS, preferred_element_type=jnp.float32
    )
    merger_up_bias_grad = jnp.sum(grad_pre_all, axis=0, dtype=jnp.float32)
    return (merger_up_grad, merger_up_bias_grad, merger_down_grad, merger_down_bias_grad)


def solution(mesh):
    in_specs = (
        P(("group", "row"), "col", None),
        P(),
        P(),
        P("col", "row"),
        P("row"),
        P("row", "col"),
        P("col"),
        P("col"),
        P("col", "row"),
        P("col", "row"),
        P(("group", "col"), "row"),
        P("group"),
        P("group"),
    )
    out_specs = (
        P(("group", "col"), "row"),
        P(("group", "row")),
        P(("group", "row"), "col"),
        P(("group", "col")),
    )
    return jax.shard_map(shards, mesh=mesh, in_specs=in_specs, out_specs=out_specs, check_vma=False)
```

profile of v0, /device:TPU:0, one launch (start us, length us, event | category | flops | bytes accessed | tf_op | source)
XLA Modules:
  0.0 698.9 jit_solution(3855103941786957547)
XLA Ops:
  7.2 0.8 convert_element_type.115
  8.0 0.8 convert_element_type.114
  8.9 1.1 convert_reduce_fusion.2
  10.0 1.2 fusion.19
  11.2 1.3 fusion.22
  12.4 0.8 copy.34
  13.3 0.7 and_select_fusion.1
  13.9 0.2 convert_reduce_fusion.3
  14.1 0.1 dynamic_slice.9
  14.2 0.1 dynamic_slice.10
  14.3 1.3 fusion.1
  15.6 1.0 copy.27
  16.6 7.4 %all-to-all-start = ((bf16[16,2,4,1280]{3,2,1,0:T(4,128)(2,1)}), bf16[16,2,4,1280]{3,2,1,0:T(4,128)(2,1)}, u32[]{:S(2)}, u32[]{:S(2)}) async-start(bf16[16,2,4,1280]{3,2,1,0:T(4,128)(2,1)} %bitcast.52), calls=%async_computation | async-start | bytes 655360 | tf_op jit(solution)/shard_map/all_to_all | solution.py:101
  24.1 11.4 %all-to-all-done = bf16[16,2,4,1280]{3,2,1,0:T(4,128)(2,1)} async-done(((bf16[16,2,4,1280]{3,2,1,0:T(4,128)(2,1)}), bf16[16,2,4,1280]{3,2,1,0:T(4,128)(2,1)}, u32[]{:S(2)}, u32[]{:S(2)}) %all-to-all-start) | async-done | bytes 327712 | tf_op jit(solution)/shard_map/all_to_all | solution.py:101
  35.5 2.3 fusion
  37.8 1.8 copy.29
  39.7 1.8 reshape.126
  41.5 17.0 %all-gather.8.cloned.1.call-done = bf16[512,1280]{1,0:T(8,128)(2,1)} async-done(((bf16[128,1280]{1,0:T(8,128)(2,1)}), bf16[512,1280]{1,0:T(8,128)(2,1)}) %all-gather.8.cloned.1.call-update) | async-done | bytes 1310736 | tf_op jit(solution)/shard_map/all_gather | solution.py:107
  58.5 4.2 convolution_convert_fusion.4
  62.8 31.3 %reduce-scatter.8.cloned.1.call-done = bf16[128,1280]{1,0:T(8,128)(2,1)} async-done(((bf16[512,1280]{1,0:T(8,128)(2,1)}), bf16[128,1280]{1,0:T(8,128)(2,1)}) %reduce-scatter.8.cloned.1.call-update) | async-done | bytes 327696 | tf_op jit(solution)/shard_map/reduce_scatter | solution.py:111
  94.1 3.1 fusion.25
  97.4 31.6 %all-gather.10.cloned.1.call-done = bf16[512,1280]{1,0:T(8,128)(2,1)} async-done(((bf16[128,1280]{1,0:T(8,128)(2,1)}), bf16[512,1280]{1,0:T(8,128)(2,1)}) %all-gather.10.cloned.1.call-update) | async-done | bytes 1310736 | tf_op jit(solution)/shard_map/all_gather | solution.py:118
  129.0 7.1 %convolution_convert_fusion.3 = bf16[512,2048]{1,0:T(8,128)(2,1)} fusion(bf16[512,1280]{1,0:T(8,128)(2,1)} %all-gather.10.cloned.1.call-done, bf16[1280,2048]{1,0:T(8,128)(2,1)} %param.18), kind=kOutput, calls=%fused_computation.6 | convolution fusion | flops 2685403136 | bytes 8650752 | tf_op jit(solution)/shard_map/dot_general | solution.py:123
  136.2 30.5 %reduce-scatter.10.cloned.1.call-done = bf16[128,2048]{1,0:T(8,128)(2,1)} async-done(((bf16[512,2048]{1,0:T(8,128)(2,1)}), bf16[128,2048]{1,0:T(8,128)(2,1)}) %reduce-scatter.10.cloned.1.call-update) | async-done | bytes 524304 | tf_op jit(solution)/shard_map/reduce_scatter | solution.py:122
  166.6 1.1 add_convert_fusion.1
  167.8 0.2 fusion.11
  168.0 11.7 %psum.14 = f32[128]{0:T(128)S(1)} all-reduce(f32[128]{0:T(128)S(1)} %fusion.11), channel_id=1, replica_groups=mesh['group'=2,'row'=4,'col'=4] {'col'}, use_global_device_ids=true, to_apply=%region_6.7 | all-reduce | flops 128 | bytes 1024 | tf_op jit(solution)/shard_map/psum | solution.py:134
  179.7 1.0 fusion.13
  180.7 0.2 reduce-scatter.16.cloned.1.call-start
  180.9 19.8 %all-gather.12.cloned.1.call-done = bf16[512,2048]{1,0:T(8,128)(2,1)} async-done(((bf16[128,2048]{1,0:T(8,128)(2,1)}), bf16[512,2048]{1,0:T(8,128)(2,1)}) %all-gather.12.cloned.1.call-update) | async-done | bytes 2097168 | tf_op jit(solution)/shard_map/all_gather | solution.py:138
  200.7 13.9 %convolution_convert_fusion = bf16[512,3696]{0,1:T(8,128)(2,1)} fusion(bf16[512,2048]{1,0:T(8,128)(2,1)} %all-gather.12.cloned.1.call-done, bf16[2048,3696]{0,1:T(8,128)(2,1)} %param.22), kind=kOutput, calls=%fused_computation.1 | convolution fusion | flops 7752966144 | bytes 21020672 | tf_op jit(solution)/shard_map/dot_general | solution.py:145
  214.5 12.7 %convolution_convert_fusion.1 = bf16[512,3696]{0,1:T(8,128)(2,1)} fusion(bf16[512,2048]{1,0:T(8,128)(2,1)S(1)} %copy-done.8, bf16[2048,3696]{0,1:T(8,128)(2,1)} %param.21), kind=kOutput, calls=%fused_computation.2 | convolution fusion | flops 7752966144 | bytes 21020672 | tf_op jit(solution)/shard_map/dot_general | solution.py:144
  227.3 6.7 pad_maximum_fusion
  234.0 10.1 %copy.35 = bf16[512,7392]{1,0:T(8,128)(2,1)} copy(bf16[512,7392]{0,1:T(8,128)(2,1)} %pad_maximum_fusion) | data formatting | bytes 15138816
  244.2 0.6 copy-done.9
  244.7 0.1 select_reduce_fusion
  244.8 0.1 iota_compare_fusion.1
  244.9 0.1 lt.47
  245.0 0.1 dynamic_slice.11
  245.1 131.2 %reduce-scatter.16.cloned.1.call-done = bf16[128,7392]{1,0:T(8,128)(2,1)} async-done(((bf16[512,7392]{1,0:T(8,128)(2,1)}), bf16[128,7392]{1,0:T(8,128)(2,1)}) %reduce-scatter.16.cloned.1.call-update) | async-done | bytes 1892368
  376.3 1.8 fusion.65
  378.1 1.3 copy.38
  379.5 1.1 copy.37
  380.6 3.8 fusion.9
  384.5 0.7 all-gather.16.cloned.1.call-update
  385.2 0.3 reduce-scatter.12.cloned.1.call-start
  385.5 73.5 %all-gather.14.cloned.1.call-done = bf16[512,3696]{0,1:T(8,128)(2,1)} async-done(((bf16[128,3696]{0,1:T(8,128)(2,1)}), bf16[512,3696]{0,1:T(8,128)(2,1)}) %all-gather.14.cloned.1.call-update) | async-done | bytes 3784720 | tf_op jit(solution)/shard_map/all_gather | solution.py:158
  459.0 14.1 %fusion.66 = f32[512,2048]{1,0:T(8,128)} fusion(bf16[512,3696]{0,1:T(8,128)(2,1)} %all-gather.14.cloned.1.call-done, bf16[2048,3696]{0,1:T(8,128)(2,1)} %param.21), kind=kOutput, calls=%fused_computation.119 | convolution fusion | flops 7751073792 | bytes 23117824 | tf_op jit(solution)/shard_map/dot_general | solution.py:161
  473.1 60.2 %all-gather.16.cloned.1.call-done = bf16[512,3696]{0,1:T(8,128)(2,1)} async-done(((bf16[128,3696]{0,1:T(8,128)(2,1)}), bf16[512,3696]{0,1:T(8,128)(2,1)}) %all-gather.16.cloned.1.call-update) | async-done | bytes 3784720 | tf_op jit(solution)/shard_map/all_gather | solution.py:159
  533.3 14.3 %add_convert_fusion = bf16[512,2048]{1,0:T(8,128)(2,1)} fusion(f32[512,2048]{1,0:T(8,128)} %fusion.66, bf16[512,3696]{0,1:T(8,128)(2,1)} %all-gather.16.cloned.1.call-done, bf16[2048,3696]{0,1:T(8,128)(2,1)} %param.22), kind=kOutput, calls=%fused_computation.4 | convolution fusion | flops 7753170944 | bytes 25214976 | tf_op jit(solution)/shard_map/dot_general | solution.py:167
  547.7 29.7 %reduce-scatter.12.cloned.1.call-done = bf16[128,2048]{1,0:T(8,128)(2,1)} async-done(((bf16[512,2048]{1,0:T(8,128)(2,1)}), bf16[128,2048]{1,0:T(8,128)(2,1)}) %reduce-scatter.12.cloned.1.call-update) | async-done | bytes 524304 | tf_op jit(solution)/shard_map/reduce_scatter | solution.py:164
  577.4 1.3 fusion.14
  578.7 11.7 %psum.15 = f32[128]{0:T(128)S(1)} all-reduce(f32[128]{0:T(128)S(1)} %fusion.14), channel_id=1, replica_groups=mesh['group'=2,'row'=4,'col'=4] {'col'}, use_global_device_ids=true, to_apply=%region_11.12 | all-reduce | flops 128 | bytes 1024 | tf_op jit(solution)/shard_map/psum | solution.py:174
  590.4 2.1 fusion.16
  592.6 19.9 %all-gather.18.cloned.1.call-done = bf16[512,2048]{1,0:T(8,128)(2,1)} async-done(((bf16[128,2048]{1,0:T(8,128)(2,1)}), bf16[512,2048]{1,0:T(8,128)(2,1)}) %all-gather.18.cloned.1.call-update) | async-done | bytes 2097168 | tf_op jit(solution)/shard_map/all_gather | solution.py:178
  612.5 7.1 %convolution_convert_fusion.2 = bf16[512,1280]{1,0:T(8,128)(2,1)} fusion(bf16[512,2048]{1,0:T(8,128)(2,1)} %all-gather.18.cloned.1.call-done, bf16[1280,2048]{1,0:T(8,128)(2,1)} %param.18), kind=kOutput, calls=%fused_computation.5 | convolution fusion | flops 2685009920 | bytes 8650752 | tf_op jit(solution)/shard_map/dot_general | solution.py:185
  619.6 0.3 all-gather.20.cloned.1.call-start
  619.9 31.1 %reduce-scatter.14.cloned.1.call-done = bf16[128,1280]{1,0:T(8,128)(2,1)} async-done(((bf16[512,1280]{1,0:T(8,128)(2,1)}), bf16[128,1280]{1,0:T(8,128)(2,1)}) %reduce-scatter.14.cloned.1.call-update) | async-done | bytes 327696 | tf_op jit(solution)/shard_map/reduce_scatter | solution.py:184
  651.0 2.0 fusion.31
  653.0 1.0 convert_reduce_fusion
  654.0 7.0 fusion.68
  661.0 23.7 %all-gather.20.cloned.1.call-done = bf16[512,1280]{1,0:T(8,128)(2,1)} async-done(((bf16[128,1280]{1,0:T(8,128)(2,1)}), bf16[512,1280]{1,0:T(8,128)(2,1)}) %all-gather.20.cloned.1.call-update) | async-done | bytes 1310736 | tf_op jit(solution)/shard_map/all_gather | solution.py:193
  684.7 6.6 fusion.67
  691.2 0.8 convert_reduce_fusion.1
  (54 shorter events, 0.7 us)
Async XLA Ops:
  7.2 51.3 %copy-start = (bf16[1280,1280]{1,0:T(8,128)(2,1)S(1)}, bf16[1280,1280]{1,0:T(8,128)(2,1)}, u32[]{:S(2)}) copy-start(bf16[1280,1280]{1,0:T(8,128)(2,1)} %param.16) | copy-start | bytes 9830404
  7.2 28.3 %copy-start.10 = (s32[32]{0:T(128)S(1)}, s32[32]{0:T(128)}, u32[]{:S(2)}) copy-start(s32[32]{0:T(128)} %param.24) | copy-start | bytes 388
  16.6 18.9 %all-to-all-start = ((bf16[16,2,4,1280]{3,2,1,0:T(4,128)(2,1)}), bf16[16,2,4,1280]{3,2,1,0:T(4,128)(2,1)}, u32[]{:S(2)}, u32[]{:S(2)}) async-start(bf16[16,2,4,1280]{3,2,1,0:T(4,128)(2,1)} %bitcast.52), calls=%async_computation | async-start | bytes 655360 | tf_op jit(solution)/shard_map/all_to_all | solution.py:101
  24.0 34.5 %all-gather.8.cloned.1.call-start = ((), (), s32[]{:S(2)}) async-start(), calls=%async_computation.6 | async-start | bytes 1638400 | tf_op jit(solution)/shard_map/all_gather | solution.py:107
  41.5 21.4 %copy-start.5 = (bf16[1280]{0:T(1024)(128)(2,1)S(1)}, bf16[1280]{0:T(1024)(128)(2,1)}, u32[]{:S(2)}) copy-start(bf16[1280]{0:T(1024)(128)(2,1)} %param.17) | copy-start | bytes 7684
  41.5 52.7 %reduce-scatter.8.cloned.1.call-start = ((), (), s32[]{:S(2)}) async-start(), calls=%async_computation.7 | async-start | bytes 1638400 | tf_op jit(solution)/shard_map/reduce_scatter | solution.py:111
  62.8 66.2 %all-gather.10.cloned.1.call-start = ((), (), s32[]{:S(2)}) async-start(), calls=%async_computation.8 | async-start | bytes 1638400 | tf_op jit(solution)/shard_map/all_gather | solution.py:118
  97.3 38.8 %copy-start.6 = (bf16[2048]{0:T(1024)(128)(2,1)S(1)}, bf16[2048]{0:T(1024)(128)(2,1)}, u32[]{:S(2)}) copy-start(bf16[2048]{0:T(1024)(128)(2,1)} %param.19) | copy-start | bytes 12292
  97.3 38.8 %copy-start.7 = (bf16[2048]{0:T(1024)(128)(2,1)S(1)}, bf16[2048]{0:T(1024)(128)(2,1)}, u32[]{:S(2)}) copy-start(bf16[2048]{0:T(1024)(128)(2,1)} %param.20) | copy-start | bytes 12292
  97.3 69.3 %reduce-scatter.10.cloned.1.call-start = ((), (), s32[]{:S(2)}) async-start(), calls=%async_computation.9 | async-start | bytes 2621440 | tf_op jit(solution)/shard_map/reduce_scatter | solution.py:122
  136.1 64.6 %all-gather.12.cloned.1.call-start = ((), (), s32[]{:S(2)}) async-start(), calls=%async_computation.10 | async-start | bytes 2621440 | tf_op jit(solution)/shard_map/all_gather | solution.py:138
  180.7 195.6 %reduce-scatter.16.cloned.1.call-start = ((), (), s32[]{:S(2)}) async-start(), calls=%async_computation.17 | async-start | bytes 9502720
  200.7 13.9 %copy-start.8 = (bf16[512,2048]{1,0:T(8,128)(2,1)S(1)}, bf16[512,2048]{1,0:T(8,128)(2,1)}, u32[]{:S(2)}) copy-start(bf16[512,2048]{1,0:T(8,128)(2,1)} %all-gather.12.cloned.1.call-done) | copy-start | bytes 6291460
  244.1 0.7 copy-start.9
  244.1 214.9 %all-gather.14.cloned.1.call-start = ((), (), s32[]{:S(2)}) async-start(), calls=%async_computation.11 | async-start | bytes 4730880 | tf_op jit(solution)/shard_map/all_gather | solution.py:158
  384.4 148.9 %all-gather.16.cloned.1.call-start = ((), (), s32[]{:S(2)}) async-start(), calls=%async_computation.12 | async-start | bytes 4730880 | tf_op jit(solution)/shard_map/all_gather | solution.py:159
  385.2 192.2 %reduce-scatter.12.cloned.1.call-start = ((), (), s32[]{:S(2)}) async-start(), calls=%async_computation.13 | async-start | bytes 2621440 | tf_op jit(solution)/shard_map/reduce_scatter | solution.py:164
  547.6 64.9 %all-gather.18.cloned.1.call-start = ((), (), s32[]{:S(2)}) async-start(), calls=%async_computation.14 | async-start | bytes 2621440 | tf_op jit(solution)/shard_map/all_gather | solution.py:178
  592.5 58.5 %copy-start.4 = (bf16[128,1280]{1,0:T(8,128)(2,1)S(1)}, bf16[128,1280]{1,0:T(8,128)(2,1)}, u32[]{:S(2)}) copy-start(bf16[128,1280]{1,0:T(8,128)(2,1)} %reduce-scatter.8.cloned.1.call-done) | copy-start | bytes 983044
  592.5 58.5 %reduce-scatter.14.cloned.1.call-start = ((), (), s32[]{:S(2)}) async-start(), calls=%async_computation.15 | async-start | bytes 1638400 | tf_op jit(solution)/shard_map/reduce_scatter | solution.py:184
  619.6 33.5 %copy-start.2 = (bf16[512,2048]{1,0:T(8,128)(2,1)S(1)}, bf16[512,2048]{1,0:T(8,128)(2,1)}, u32[]{:S(2)}) copy-start(bf16[512,2048]{1,0:T(8,128)(2,1)} %all-gather.18.cloned.1.call-done) | copy-start | bytes 6291460
  619.6 65.1 %all-gather.20.cloned.1.call-start = ((), (), s32[]{:S(2)}) async-start(), calls=%async_computation.16 | async-start | bytes 1638400 | tf_op jit(solution)/shard_map/all_gather | solution.py:193
  684.7 6.6 copy-start.3
  684.7 7.4 %copy-start.1 = (bf16[1280,1280]{1,0:T(8,128)(2,1)S(1)}, bf16[1280,1280]{1,0:T(8,128)(2,1)}, u32[]{:S(2)}) copy-start(bf16[1280,1280]{1,0:T(8,128)(2,1)} %param.16) | copy-start | bytes 9830404
Sparse Core Ops, SparseCore 0:
  41.6 16.8 all-gather.7
  62.9 31.2 reduce-scatter.7
  97.4 31.4 all-gather.9
  136.2 30.4 reduce-scatter.9
  180.8 19.8 all-gather.11
  244.2 132.0 reduce-scatter.15
  384.6 74.3 all-gather.13
  461.2 72.0 all-gather.15
  547.7 29.6 reduce-scatter.11
  592.6 19.8 all-gather.17
  619.7 31.2 reduce-scatter.13
  653.1 31.4 all-gather.19
where the time goes:
time: 700 us; the launch traced here: 699 us
  waiting for transfers between devices  512 us (73%)
  matrix products  90.5 us (13%)
  other arithmetic  29.5 us (4%)
  blocking collectives  23.4 us (3%)
  local copies, waits for them, and re-layouts  20.7 us (3%)
  between operations  14.4 us (2%)
  starting transfers between devices  8.57 us (1%)
    unnamed x13, waiting for transfers between devices  132 us
    all_gather x1, waiting for transfers between devices, shards(): lax.all_gather(grad_gate, 'col', axis=0, tiled=True)  73.5 us
    all_gather x1, waiting for transfers between devices, shards(): lax.all_gather(grad_up, 'col', axis=0, tiled=True)  60.2 us
    all_gather x1, waiting for transfers between devices, shards(): hidden_all = lax.all_gather(hidden_one, 'col', axis=0, tiled=True)  31.6 us
    reduce_scatter x1, waiting for transfers between devices, shards(): lax.psum_scatter(jnp.dot(rows_part, merger_up, preferred_element_type=jnp...  31.3 us
    reduce_scatter x1, waiting for transfers between devices, shards(): lax.psum_scatter(lax.dot_general(rows_part, merger_down, CONTRACT_COLS, p...  31.1 us
    reduce_scatter x1, waiting for transfers between devices, shards(): lax.psum_scatter(jnp.dot(rows_part, merger_down, preferred_element_type=j...  30.5 us
    reduce_scatter x1, waiting for transfers between devices, shards(): lax.psum_scatter((from_gate + lax.dot_general(grad_up_all, w_up, CONTRACT...  29.7 us
  transfers between devices with their start and end apart: 13, of which 13 were waited for; matrix products, arithmetic and copies ran while one was open for 3% of the time, Pallas kernels for 0%

commit v1 on v0

v1 whole, which is shorter than its diff:
```python
import functools
import math

import jax
import jax.numpy as jnp
from jax import lax
from jax.sharding import PartitionSpec as P

D = 8192
BLK = 16
IMG_ROW = 8


EPS_PATCH = 1e-06
EPS_NORM = 1e-06
CONTRACT_ROWS = (((0,), (0,)), ((), ()))
CONTRACT_COLS = (((1,), (1,)), ((), ()))


def gelu_slope(inputs):
    cumulative = 0.5 * (1.0 + jax.scipy.special.erf(inputs / math.sqrt(2.0)))
    return cumulative + inputs * jnp.exp(-0.5 * inputs * inputs) / math.sqrt(2.0 * math.pi)


def patch_tokens(patches, patch_gain, patch_bias):
    values = patches.astype(jnp.float32)
    center = values - jnp.mean(values, axis=-1, keepdims=True)
    spread = jnp.mean(center * center, axis=-1, keepdims=True)
    normed = center * lax.rsqrt(spread + EPS_PATCH) * patch_gain.astype(
        jnp.float32
    ) + patch_bias.astype(jnp.float32)
    image_count, patch_slots, patch_width = patches.shape
    return normed.astype(jnp.bfloat16).reshape(image_count, patch_slots // 4, 4 * patch_width)


def swiglu_grads(gate_out, up_out, cotangent):
    gate_f = gate_out.astype(jnp.float32)
    up_f = up_out.astype(jnp.float32)
    masked = cotangent.astype(jnp.float32)
    logistic = jax.nn.sigmoid(gate_f)
    grad_gate = (masked * up_f * logistic * (1.0 + gate_f * (1.0 - logistic))).astype(jnp.bfloat16)
    grad_up = (masked * gate_f * logistic).astype(jnp.bfloat16)
    return (grad_gate, grad_up)


def pack_plan(placement, patch_counts, tokens, n_row, n_col, cap):
    images = placement.shape[0]
    rows = tokens // n_col
    blocks = rows // BLK
    ids = jnp.arange(images, dtype=jnp.int32)
    cols = jnp.arange(n_col, dtype=jnp.int32)
    hit = placement[:, None] == ids[None, :]
    fill = jnp.sum(jnp.where(hit, (patch_counts // 4)[:, None], 0), axis=0)
    owner = ids // blocks
    before = (owner[:, None] == owner[None, :]) & (ids[None, :] < ids[:, None])
    start = jnp.sum(jnp.where(before, fill[None, :], 0), axis=1)
    count = jnp.sum(jnp.where(owner[None, :] == cols[:, None], fill[None, :], 0), axis=1)
    over = jnp.maximum(count - cap, 0)
    free = jnp.maximum(cap - count, 0)
    lower = cols[None, :] < cols[:, None]
    over_start = jnp.sum(jnp.where(lower, over[None, :], 0), axis=1)
    free_start = jnp.sum(jnp.where(lower, free[None, :], 0), axis=1)

    def spill_slot(number):
        inside = (number[..., None] >= free_start) & (number[..., None] < free_start + free)
        return jnp.sum(
            jnp.where(inside, cols * cap + count + number[..., None] - free_start, 0), axis=-1
        )

    place = jnp.arange(BLK, dtype=jnp.int32)
    rank = start[:, None] + place[None, :]
    real = place[None, :] < fill[:, None]
    owner_over = jnp.sum(jnp.where(owner[:, None] == cols[None, :], over_start[None, :], 0), axis=1)
    slot = jnp.where(
        rank < cap,
        owner[:, None] * cap + rank,
        spill_slot(owner_over[:, None] + rank - cap),
    )
    slot = jnp.where(real, slot, -1)
    rank = jnp.where(real, rank, -1)
    by_image = jnp.sum(jnp.where(hit[:, :, None], slot[None, :, :], 0), axis=1)
    extra = jnp.arange(rows - cap, dtype=jnp.int32)
    extra_slot = jnp.where(
        extra[None, :] < over[:, None], spill_slot(over_start[:, None] + extra[None, :]), -1
    )
    return slot.reshape(-1), rank.reshape(-1), by_image, extra_slot.reshape(-1)


def one_hot(slots, first, size):
    return (slots[None, :] - first == jnp.arange(size, dtype=jnp.int32)[:, None]).astype(
        jnp.bfloat16
    )


def pick(selection, values):
    return jnp.dot(selection, values, preferred_element_type=jnp.float32)


def packed_step(cap, sequence_in, operands):
    (
        merger_up,
        merger_up_bias,
        merger_down,
        merger_down_bias,
        norm_gain,
        w_gate,
        w_up,
        hidden_cotangent,
        placement,
        patch_counts,
    ) = operands
    n_row = lax.axis_size("row")
    n_col = lax.axis_size("col")
    row_index = lax.axis_index("row")
    col_index = lax.axis_index("col")
    tokens = sequence_in.shape[0]
    held = hidden_cotangent.shape[0]
    packed = cap * n_col
    rows_row = packed // n_row
    slot, rank, by_image, extra_slot = pack_plan(
        placement, patch_counts, tokens, n_row, n_col, cap
    )
    arrival = by_image.reshape(n_row, IMG_ROW, n_col, BLK // n_col)
    arrival = jnp.transpose(arrival, (0, 2, 1, 3)).reshape(-1)
    sequence = pick(one_hot(arrival, 0, packed), sequence_in).astype(jnp.bfloat16)
    slot_here = lax.dynamic_slice_in_dim(slot, col_index * held, held)
    cotangent = pick(one_hot(slot_here, col_index * cap, cap), hidden_cotangent)
    if cap < held:
        rank_here = lax.dynamic_slice_in_dim(rank, col_index * held, held)
        spilled = pick(one_hot(rank_here, cap, held - cap), hidden_cotangent).astype(jnp.bfloat16)
        spilled_all = lax.all_gather(spilled, "col", axis=0, tiled=True)
        cotangent = cotangent + pick(one_hot(extra_slot, col_index * cap, cap), spilled_all)
    cotangent = cotangent.astype(jnp.bfloat16)

    pre_act = lax.psum_scatter(
        pick(sequence, merger_up).astype(jnp.bfloat16), "col", scatter_dimension=0, tiled=True
    ).astype(jnp.float32) + merger_up_bias.astype(jnp.float32)
    hidden_one = jax.nn.gelu(pre_act, approximate=False).astype(jnp.bfloat16)
    hidden_all = lax.all_gather(hidden_one, "col", axis=0, tiled=True)
    merged_out = lax.optimization_barrier(
        (
            lax.psum_scatter(
                pick(hidden_all, merger_down).astype(jnp.bfloat16),
                "row",
                scatter_dimension=0,
                tiled=True,
            ).astype(jnp.float32)
            + merger_down_bias.astype(jnp.float32)
        ).astype(jnp.bfloat16)
    )

    def row_sums(part):
        spread = jnp.where(
            jnp.arange(n_row, dtype=jnp.int32)[:, None] == row_index, part[None, :], 0.0
        )
        return lax.psum(spread.reshape(-1), ("row", "col"))

    merged_f = merged_out.astype(jnp.float32)
    merged_all = lax.all_gather(merged_out, "row", axis=0, tiled=True).astype(jnp.float32)
    square_sums = row_sums(jnp.sum(merged_f * merged_f, axis=1))
    inv_rms = lax.rsqrt(square_sums / D + EPS_NORM)
    gain = norm_gain.astype(jnp.float32)
    normed_all = (merged_all * inv_rms[:, None] * gain).astype(jnp.bfloat16)

    def gate_sums(weight):
        return lax.psum_scatter(
            pick(normed_all, weight).astype(jnp.bfloat16), "col", scatter_dimension=0, tiled=True
        )

    gate_out = gate_sums(w_gate)
    up_out = gate_sums(w_up)
    grad_gate, grad_up = swiglu_grads(gate_out, up_out, cotangent)
    grad_gate_all = lax.all_gather(grad_gate, "col", axis=0, tiled=True)
    grad_up_all = lax.all_gather(grad_up, "col", axis=0, tiled=True)
    from_gate = lax.dot_general(
        grad_gate_all, w_gate, CONTRACT_COLS, preferred_element_type=jnp.float32
    )
    grad_normed = lax.psum_scatter(
        (
            from_gate
            + lax.dot_general(grad_up_all, w_up, CONTRACT_COLS, preferred_element_type=jnp.float32)
        ).astype(jnp.bfloat16),
        "row",
        scatter_dimension=0,
        tiled=True,
    )
    inner = row_sums(jnp.sum(merged_f * (gain * grad_normed.astype(jnp.float32)), axis=1))
    gained_all = gain * lax.all_gather(grad_normed, "row", axis=0, tiled=True).astype(jnp.float32)
    grad_merged_all = (
        inv_rms[:, None] * gained_all
        - merged_all * (inv_rms * inv_rms * inv_rms / D * inner)[:, None]
    ).astype(jnp.bfloat16)
    grad_hidden = lax.psum_scatter(
        lax.dot_general(
            grad_merged_all, merger_down, CONTRACT_COLS, preferred_element_type=jnp.float32
        ).astype(jnp.bfloat16),
        "col",
        scatter_dimension=0,
        tiled=True,
    ).astype(jnp.float32)
    merger_down_grad = lax.dot_general(
        hidden_all, grad_merged_all, CONTRACT_ROWS, preferred_element_type=jnp.float32
    )
    merger_down_bias_grad = jnp.sum(grad_merged_all, axis=0, dtype=jnp.float32)
    grad_pre = (grad_hidden * gelu_slope(pre_act)).astype(jnp.bfloat16)
    grad_pre_all = lax.all_gather(grad_pre, "col", axis=0, tiled=True)
    merger_up_grad = lax.dot_general(
        sequence, grad_pre_all, CONTRACT_ROWS, preferred_element_type=jnp.float32
    )
    merger_up_bias_grad = jnp.sum(grad_pre_all, axis=0, dtype=jnp.float32)
    return (merger_up_grad, merger_up_bias_grad, merger_down_grad, merger_down_bias_grad)


def shards(
    patches,
    patch_gain,
    patch_bias,
    merger_up,
    merger_up_bias,
    merger_down,
    merger_down_bias,
    norm_gain,
    w_gate,
    w_up,
    hidden_cotangent,
    placement,
    patch_counts,
):
    n_col = lax.axis_size("col")
    held = hidden_cotangent.shape[0]
    real_rows = lax.pmax(jnp.sum(patch_counts // 4), "group")
    caps = [held * 5 // 8, held * 3 // 4, held]
    branch = sum((real_rows > cap * n_col).astype(jnp.int32) for cap in caps[:-1])
    image_tokens = patch_tokens(patches, patch_gain, patch_bias)
    slot_count = image_tokens.shape[1]
    feat_width = image_tokens.shape[2] // n_col
    sending = image_tokens.reshape(IMG_ROW * slot_count, n_col, feat_width)
    sending = jnp.transpose(sending, (1, 0, 2))
    received = lax.all_to_all(sending, "col", split_axis=0, concat_axis=0, tiled=True)
    merged = received.reshape(n_col * IMG_ROW * slot_count, feat_width)
    gathered_in = lax.all_gather(merged, "row", axis=0, tiled=True)
    operands = (
        merger_up,
        merger_up_bias,
        merger_down,
        merger_down_bias,
        norm_gain,
        w_gate,
        w_up,
        hidden_cotangent,
        placement,
        patch_counts,
    )
    return lax.switch(
        branch, [functools.partial(packed_step, cap) for cap in caps], gathered_in, operands
    )


def solution(mesh):
    in_specs = (
        P(("group", "row"), "col", None),
        P(),
        P(),
        P("col", "row"),
        P("row"),
        P("row", "col"),
        P("col"),
        P("col"),
        P("col", "row"),
        P("col", "row"),
        P(("group", "col"), "row"),
        P("group"),
        P("group"),
    )
    out_specs = (
        P(("group", "col"), "row"),
        P(("group", "row")),
        P(("group", "row"), "col"),
        P(("group", "col")),
    )
    return jax.shard_map(shards, mesh=mesh, in_specs=in_specs, out_specs=out_specs, check_vma=False)
```

time: 700 us -> 544 us (0.78); the launches traced: 699 us -> 535 us
  waiting for transfers between devices: 512 us -> 277 us
  blocking collectives: 23.4 us -> 124 us
  local copies, waits for them, and re-layouts: 20.7 us -> 2.47 us
  other arithmetic: 29.5 us -> 18.5 us
  loops' own time: 0 us -> 8.88 us
  starting transfers between devices: 8.57 us -> 0.83 us
    all_gather x6 -> x5, waiting for transfers between devices: 229 us -> 91.3 us  [the longest x1 49.7 us: packed_step(): grad_gate_all = lax.all_gather(grad_gate, 'col', axis=0, tiled=True)]
    unnamed x13 -> x1, waiting for transfers between devices: 132 us -> 0.02 us
    reduce_scatter x4 -> x6, waiting for transfers between devices: 123 us -> 174 us  [the longest x2 83 us: gate_sums(): lax.psum_scatter(pick(normed_all, weight).astype(jnp.bfloat16), 'col', sc...]
    psum x2, blocking collectives: 23.4 us -> 65.7 us  [row_sums(): return lax.psum(spread.reshape(-1), ('row', 'col'))]
    all_gather x0 -> x2, blocking collectives: none -> 36.8 us  [the longest x1 18.4 us: packed_step(): hidden_all = lax.all_gather(hidden_one, 'col', axis=0, tiled=True)]
    all_to_all x0 -> x1, blocking collectives: none -> 16.5 us  [shards(): lax.all_to_all(sending, 'col', split_axis=0, concat_axis=0, tiled=True)]
    unnamed x25 -> x12, local copies, waits for them, and re-layouts: 13.2 us -> 0.03 us
    all_to_all x1 -> x0, waiting for transfers between devices: 11.4 us -> none  [shards(): lax.all_to_all(sending, ('row', 'col'), split_axis=0, concat_axis=0, tile...]
  transfers between devices with their start and end apart: 13 -> 12, of which waited for: 13 -> 9; matrix products, arithmetic and copies ran while one was open for 3% -> 11% of each run, Pallas kernels for 0% -> 0%
where the time goes in v1:
time: 544 us; the launch traced here: 535 us
  waiting for transfers between devices  277 us (51%)
  blocking collectives  124 us (23%)
  matrix products  87.7 us (16%)
  other arithmetic  18.5 us (3%)
  between operations  15.7 us (3%)
  loops' own time  8.88 us (2%)
    reduce_scatter x2, waiting for transfers between devices, gate_sums(): lax.psum_scatter(pick(normed_all, weight).astype(jnp.bfloat16), 'col', sc...  83 us
    psum x2, blocking collectives, row_sums(): return lax.psum(spread.reshape(-1), ('row', 'col'))  65.7 us
    dot_general x8, matrix products, pick(): return jnp.dot(selection, values, preferred_element_type=jnp.float32)  51.3 us
    all_gather x1, waiting for transfers between devices, packed_step(): grad_gate_all = lax.all_gather(grad_gate, 'col', axis=0, tiled=True)  49.7 us
    all_gather x1, waiting for transfers between devices, packed_step(): grad_up_all = lax.all_gather(grad_up, 'col', axis=0, tiled=True)  41.6 us
    reduce_scatter x1, waiting for transfers between devices, packed_step(): lax.psum_scatter(pick(hidden_all, merger_down).astype(jnp.bfloat16), 'row...  26 us
    reduce_scatter x1, waiting for transfers between devices, packed_step(): lax.psum_scatter((from_gate + lax.dot_general(grad_up_all, w_up, CONTRACT...  25.4 us
    reduce_scatter x1, waiting for transfers between devices, packed_step(): lax.psum_scatter(pick(sequence, merger_up).astype(jnp.bfloat16), 'col', s...  23.7 us
  transfers between devices with their start and end apart: 12, of which 9 were waited for; matrix products, arithmetic and copies ran while one was open for 11% of the time, Pallas kernels for 0%

profile of v1, /device:TPU:0, one launch (start us, length us, event | category | flops | bytes accessed | tf_op | source)
XLA Modules:
  0.0 535.2 jit_solution(16696869693114893061)
XLA Ops:
  7.3 1.2 convert_reduce_fusion.6
  8.4 1.2 fusion.140
  9.6 0.7 convert_element_type.307
  10.4 0.7 convert_element_type.308
  11.0 1.2 fusion.143
  12.3 0.1 reshape_reshape.3
  12.4 16.5 %all_to_all.5 = bf16[4,32,1280]{2,1,0:T(8,128)(2,1)} all-to-all(bf16[4,32,1280]{2,1,0:T(8,128)(2,1)S(1)} %bitcast.84), channel_id=1, replica_groups=mesh['group'=2,'row'=4,'col'=4] {'col'}, dimensions={0} | all-to-all | bytes 655360 | tf_op jit(solution)/shard_map/all_to_all | solution.py:239
  29.0 0.6 fusion.144
  29.6 4.9 pmax.7
  35.8 10.6 %all-gather.47.cloned.1.call-done = bf16[512,1280]{1,0:T(8,128)(2,1)} async-done(((bf16[128,1280]{1,0:T(8,128)(2,1)}), bf16[512,1280]{1,0:T(8,128)(2,1)}) %all-gather.47.cloned.1.call-update) | async-done | bytes 1310736 | tf_op jit(solution)/shard_map/all_gather | solution.py:241
  46.4 481.6 %conditional.1 = (f32[1280,1280]{1,0:T(8,128)}, f32[1280]{0:T(1024)}, f32[1280,2048]{1,0:T(8,128)}, f32[2048]{0:T(1024)}) conditional(s32[]{:T(128)} %clamp.3, (s32[32]{0:T(128)S(1)}, s32[32]{0:T(128)S(1)}, bf16[512,1280]{1,0:T(8,128)(2,1)}, bf16[1280,1280]{1,0:T(8,128)(2,1)}, bf16[1280]{0:T(1024)(128)(2,1)S(1)}, ...), branch_computations={%region_4.26_spmd, %region_26.48_spmd, %region_48.69_spmd} | conditional | flops 43257413632 | bytes 329811552 | solution.py:254
  46.5 0.1 select_reduce_fusion.3
  46.6 0.1 select_reduce_fusion.8
  46.7 0.2 select_reduce_fusion.2
  47.0 0.1 select_reduce_fusion.5
  47.1 0.1 select_reduce_fusion.7
  47.2 0.1 select_reduce_fusion.6
  47.3 0.1 select_reduce_fusion.1
  47.5 0.6 select_reduce_fusion
  48.1 0.1 reshape.758
  48.2 0.2 copy.66
  48.4 0.1 eq.178
  48.5 1.9 convolution_convert_fusion.3
  50.5 1.0 copy-done.12
  51.4 4.0 convolution_convert_fusion.6
  55.6 23.7 %reduce-scatter.23.cloned.1.call-done = bf16[80,1280]{1,0:T(8,128)(2,1)} async-done(((bf16[320,1280]{1,0:T(8,128)(2,1)}), bf16[80,1280]{1,0:T(8,128)(2,1)}) %reduce-scatter.23.cloned.1.call-update) | async-done | bytes 204816 | tf_op jit(solution)/shard_map/cond/branch_0_fun/reduce_scatter | solution.py:135
  79.3 1.8 fusion.19
  81.1 18.4 %all_gather.42 = bf16[320,1280]{1,0:T(8,128)(2,1)S(1)} all-gather(bf16[80,1280]{1,0:T(8,128)(2,1)S(1)} %fusion.19), channel_id=1, replica_groups=mesh['group'=2,'row'=4,'col'=4] {'col'}, dimensions={0}, use_global_device_ids=true | all-gather | bytes 1024000 | tf_op jit(solution)/shard_map/cond/branch_0_fun/all_gather | solution.py:139
  99.5 5.4 %convolution_convert_fusion.5 = bf16[320,2048]{1,0:T(8,128)(2,1)} fusion(bf16[320,1280]{1,0:T(8,128)(2,1)S(1)} %all_gather.42, bf16[1280,2048]{1,0:T(8,128)(2,1)} %get-tuple-element.71), kind=kOutput, calls=%fused_computation.12 | convolution fusion | flops 1678376960 | bytes 7372800 | tf_op jit(solution)/shard_map/cond/branch_0_fun/dot_general | solution.py:96
  105.1 26.0 %reduce-scatter.25.cloned.1.call-done = bf16[80,2048]{1,0:T(8,128)(2,1)} async-done(((bf16[320,2048]{1,0:T(8,128)(2,1)}), bf16[80,2048]{1,0:T(8,128)(2,1)}) %reduce-scatter.25.cloned.1.call-update) | async-done | bytes 327696 | tf_op jit(solution)/shard_map/cond/branch_0_fun/reduce_scatter | solution.py:142
  131.1 1.7 add_convert_fusion
  133.0 0.1 copy.67
  133.1 0.1 lt.247
  133.3 0.1 add.488
  133.7 1.2 convolution_convert_fusion.2
  135.0 1.1 fusion.15
  136.2 0.1 select_n.253
  136.3 32.9 %psum.36 = f32[320]{0:T(512)S(1)} all-reduce(f32[320]{0:T(512)S(1)} %select_n.253), channel_id=1, replica_groups=mesh['group'=2,'row'=4,'col'=4] {'row','col'}, use_global_device_ids=true, to_apply=%region_16.16 | all-reduce | flops 320 | bytes 2560 | tf_op jit(solution)/shard_map/cond/branch_0_fun/psum | solution.py:156
  169.3 17.2 %convolution_convert_fusion = bf16[320,3696]{1,0:T(8,128)(2,1)} fusion(bf16[2048,3696]{0,1:T(8,128)(2,1)} %get-tuple-element.216, bf16[320,2048]{1,0:T(8,128)(2,1)} %all-gather.19.cloned.1.call-done, f32[2048]{0:T(1024)S(1)} %convert_element_type.216, f32[320]{0:T(512)S(1)} %add_rsqrt_fusion), kind=kOutput, calls=%fused_computation | convolution fusion | flops 4848225280 | bytes 18824448 | tf_op jit(solution)/shard_map/cond/branch_0_fun/dot_general | solution.py:96
  186.5 0.4 reduce-scatter.27.cloned.1.call-start
  186.9 16.7 %convolution_convert_fusion.1 = bf16[320,3696]{1,0:T(8,128)(2,1)} fusion(bf16[2048,3696]{0,1:T(8,128)(2,1)} %get-tuple-element.215, bf16[320,2048]{1,0:T(8,128)(2,1)S(1)} %copy-done.10, f32[2048]{0:T(1024)S(1)} %convert_element_type.216, f32[320]{0:T(512)S(1)} %add_rsqrt_fusion), kind=kOutput, calls=%fused_computation.1 | convolution fusion | flops 4848225280 | bytes 18824448 | tf_op jit(solution)/shard_map/cond/branch_0_fun/dot_general | solution.py:96
  203.8 0.1 select_reduce_fusion.4
  203.9 0.1 sub.175
  204.1 1.7 fusion.39
  205.8 32.1 %reduce-scatter.29.cloned.1.call-done = bf16[80,3696]{1,0:T(8,128)(2,1)} async-done(((bf16[320,3696]{1,0:T(8,128)(2,1)}), bf16[80,3696]{1,0:T(8,128)(2,1)}) %reduce-scatter.29.cloned.1.call-update) | async-done | bytes 591376 | tf_op jit(solution)/shard_map/cond/branch_0_fun/reduce_scatter | solution.py:166
  237.8 51.0 %reduce-scatter.27.cloned.1.call-done = bf16[80,3696]{1,0:T(8,128)(2,1)} async-done(((bf16[320,3696]{1,0:T(8,128)(2,1)}), bf16[80,3696]{1,0:T(8,128)(2,1)}) %reduce-scatter.27.cloned.1.call-update) | async-done | bytes 591376 | tf_op jit(solution)/shard_map/cond/branch_0_fun/reduce_scatter | solution.py:166
  288.8 3.0 fusion.14
  291.9 0.7 all-gather.23.cloned.1.call-update
  292.7 49.7 %all-gather.21.cloned.1.call-done = bf16[320,3696]{1,0:T(8,128)(2,1)} async-done(((bf16[80,3696]{1,0:T(8,128)(2,1)}), bf16[320,3696]{1,0:T(8,128)(2,1)}) %all-gather.21.cloned.1.call-update) | async-done | bytes 2365456 | tf_op jit(solution)/shard_map/cond/branch_0_fun/all_gather | solution.py:173
  342.3 10.3 %fusion.148 = f32[320,2048]{1,0:T(8,128)} fusion(bf16[320,3696]{1,0:T(8,128)(2,1)} %all-gather.21.cloned.1.call-done, bf16[2048,3696]{0,1:T(8,128)(2,1)} %get-tuple-element.216), kind=kOutput, calls=%fused_computation.363 | convolution fusion | flops 4844421120 | bytes 20125696 | tf_op jit(solution)/shard_map/cond/branch_0_fun/dot_general | solution.py:175
  352.6 41.6 %all-gather.23.cloned.1.call-done = bf16[320,3696]{1,0:T(8,128)(2,1)} async-done(((bf16[80,3696]{1,0:T(8,128)(2,1)}), bf16[320,3696]{1,0:T(8,128)(2,1)}) %all-gather.23.cloned.1.call-update) | async-done | bytes 2365456 | tf_op jit(solution)/shard_map/cond/branch_0_fun/all_gather | solution.py:174
  394.2 10.5 %fusion.2 = bf16[320,2048]{1,0:T(8,128)(2,1)} fusion(f32[320,2048]{1,0:T(8,128)} %fusion.148, bf16[320,3696]{1,0:T(8,128)(2,1)} %all-gather.23.cloned.1.call-done, bf16[2048,3696]{0,1:T(8,128)(2,1)} %get-tuple-element.215), kind=kOutput, calls=%fused_computation.10 | convolution fusion | flops 4845731840 | bytes 21436416 | tf_op jit(solution)/shard_map/cond/branch_0_fun/dot_general | solution.py:181
  404.8 25.4 %reduce-scatter.31.cloned.1.call-done = bf16[80,2048]{1,0:T(8,128)(2,1)} async-done(((bf16[320,2048]{1,0:T(8,128)(2,1)}), bf16[80,2048]{1,0:T(8,128)(2,1)}) %reduce-scatter.31.cloned.1.call-update) | async-done | bytes 327696 | tf_op jit(solution)/shard_map/cond/branch_0_fun/reduce_scatter | solution.py:178
  430.3 1.2 fusion.16
  431.6 0.1 select_n.262
  431.7 32.7 %psum.37 = f32[320]{0:T(512)S(1)} all-reduce(f32[320]{0:T(512)S(1)} %select_n.262), channel_id=1, replica_groups=mesh['group'=2,'row'=4,'col'=4] {'row','col'}, use_global_device_ids=true, to_apply=%region_22.22 | all-reduce | flops 320 | bytes 2560 | tf_op jit(solution)/shard_map/cond/branch_0_fun/psum | solution.py:156
  464.4 3.0 convert_reduce_fusion
  467.4 5.3 convolution_convert_fusion.4
  472.8 5.7 %fusion.150 = f32[1280,2048]{1,0:T(8,128)} fusion(bf16[320,1280]{1,0:T(8,128)(2,1)S(1)} %all_gather.42, bf16[320,2048]{1,0:T(8,128)(2,1)S(1)} %get-tuple-element.240), kind=kOutput, calls=%fused_computation.365 | convolution fusion | flops 1677721600 | bytes 12615680 | tf_op jit(solution)/shard_map/cond/branch_0_fun/dot_general | solution.py:201
  478.4 16.2 %reduce-scatter.33.cloned.1.call-done = bf16[80,1280]{1,0:T(8,128)(2,1)} async-done(((bf16[320,1280]{1,0:T(8,128)(2,1)}), bf16[80,1280]{1,0:T(8,128)(2,1)}) %reduce-scatter.33.cloned.1.call-update) | async-done | bytes 204816 | tf_op jit(solution)/shard_map/cond/branch_0_fun/reduce_scatter | solution.py:193
  494.6 1.1 fusion.25
  495.7 18.4 %all_gather.48 = bf16[320,1280]{1,0:T(8,128)(2,1)S(1)} all-gather(bf16[80,1280]{1,0:T(8,128)(2,1)S(1)} %fusion.25), channel_id=1, replica_groups=mesh['group'=2,'row'=4,'col'=4] {'col'}, dimensions={0}, use_global_device_ids=true | all-gather | bytes 1024000 | tf_op jit(solution)/shard_map/cond/branch_0_fun/all_gather | solution.py:206
  514.1 0.7 convert_reduce_fusion.1
  514.9 4.7 fusion.149
  (77 shorter events, 1.8 us)
Async XLA Ops:
  7.2 21.8 %copy-start.33 = (s32[32]{0:T(128)S(1)}, s32[32]{0:T(128)}, u32[]{:S(2)}) copy-start(s32[32]{0:T(128)} %param.28) | copy-start | bytes 388
  7.2 39.2 %copy-start.19 = (s32[32]{0:T(128)S(1)}, s32[32]{0:T(128)}, u32[]{:S(2)}) copy-start(s32[32]{0:T(128)} %param.27) | copy-start | bytes 388
  7.2 39.2 %copy-start = (bf16[128,3696]{0,1:T(8,128)(2,1)S(1)}, bf16[128,3696]{0,1:T(8,128)(2,1)}, u32[]{:S(2)}) copy-start(bf16[128,3696]{0,1:T(8,128)(2,1)} %param.26) | copy-start | bytes 2838532
  7.2 39.2 %copy-start.18 = (bf16[2048]{0:T(1024)(128)(2,1)S(1)}, bf16[2048]{0:T(1024)(128)(2,1)}, u32[]{:S(2)}) copy-start(bf16[2048]{0:T(1024)(128)(2,1)} %param.23) | copy-start | bytes 12292
  7.2 39.2 %copy-start.17 = (bf16[2048]{0:T(1024)(128)(2,1)S(1)}, bf16[2048]{0:T(1024)(128)(2,1)}, u32[]{:S(2)}) copy-start(bf16[2048]{0:T(1024)(128)(2,1)} %param.22) | copy-start | bytes 12292
  7.2 39.2 %copy-start.16 = (bf16[1280]{0:T(1024)(128)(2,1)S(1)}, bf16[1280]{0:T(1024)(128)(2,1)}, u32[]{:S(2)}) copy-start(bf16[1280]{0:T(1024)(128)(2,1)} %param.20) | copy-start | bytes 7684
  7.2 39.2 %all-gather.47.cloned.1.call-start = ((), (), s32[]{:S(2)}) async-start(), calls=%async_computation.52 | async-start | bytes 1638400 | tf_op jit(solution)/shard_map/all_gather | solution.py:241
  46.4 32.9 %reduce-scatter.23.cloned.1.call-start = ((), (), s32[]{:S(2)}) async-start(), calls=%async_computation.19 | async-start | bytes 1024000 | tf_op jit(solution)/shard_map/cond/branch_0_fun/reduce_scatter | solution.py:135
  50.4 1.0 copy-start.12
  55.5 75.6 %reduce-scatter.25.cloned.1.call-start = ((), (), s32[]{:S(2)}) async-start(), calls=%async_computation.20 | async-start | bytes 1638400 | tf_op jit(solution)/shard_map/cond/branch_0_fun/reduce_scatter | solution.py:142
  105.0 64.2 %all-gather.19.cloned.1.call-start = ((), (), s32[]{:S(2)}) async-start(), calls=%async_computation.22 | async-start | bytes 1638400 | tf_op jit(solution)/shard_map/cond/branch_0_fun/all_gather | solution.py:159
  132.9 71.2 %all-gather.17.cloned.1.call-start = ((), (), s32[]{:S(2)}) async-start(), calls=%async_computation.21 | async-start | bytes 1781760 | tf_op jit(solution)/shard_map/cond/branch_0_fun/all_gather | solution.py:131
  134.9 102.9 %reduce-scatter.29.cloned.1.call-start = ((), (), s32[]{:S(2)}) async-start(), calls=%async_computation.24 | async-start | bytes 2969600 | tf_op jit(solution)/shard_map/cond/branch_0_fun/reduce_scatter | solution.py:166
  169.2 17.6 %copy-start.10 = (bf16[320,2048]{1,0:T(8,128)(2,1)S(1)}, bf16[320,2048]{1,0:T(8,128)(2,1)}, u32[]{:S(2)}) copy-start(bf16[320,2048]{1,0:T(8,128)(2,1)} %all-gather.19.cloned.1.call-done) | copy-start | bytes 3932164 | tf_op jit(solution)/shard_map/cond
  186.5 102.4 %reduce-scatter.27.cloned.1.call-start = ((), (), s32[]{:S(2)}) async-start(), calls=%async_computation.23 | async-start | bytes 2969600 | tf_op jit(solution)/shard_map/cond/branch_0_fun/reduce_scatter | solution.py:166
  203.6 138.7 %all-gather.21.cloned.1.call-start = ((), (), s32[]{:S(2)}) async-start(), calls=%async_computation.25 | async-start | bytes 2969600 | tf_op jit(solution)/shard_map/cond/branch_0_fun/all_gather | solution.py:173
  291.9 102.3 %all-gather.23.cloned.1.call-start = ((), (), s32[]{:S(2)}) async-start(), calls=%async_computation.26 | async-start | bytes 2969600 | tf_op jit(solution)/shard_map/cond/branch_0_fun/all_gather | solution.py:174
  292.6 137.6 %reduce-scatter.31.cloned.1.call-start = ((), (), s32[]{:S(2)}) async-start(), calls=%async_computation.27 | async-start | bytes 1638400 | tf_op jit(solution)/shard_map/cond/branch_0_fun/reduce_scatter | solution.py:178
  352.6 77.7 %copy-start.3 = (bf16[80,2048]{1,0:T(8,128)(2,1)S(1)}, bf16[80,2048]{1,0:T(8,128)(2,1)}, u32[]{:S(2)}) copy-start(bf16[80,2048]{1,0:T(8,128)(2,1)} %add_convert_fusion) | copy-start | bytes 983044 | tf_op jit(solution)/shard_map/cond
  404.7 59.7 %all-gather.25.cloned.1.call-start = ((), (), s32[]{:S(2)}) async-start(), calls=%async_computation.28 | async-start | bytes 1638400 | tf_op jit(solution)/shard_map/cond/branch_0_fun/all_gather | solution.py:188
  430.3 64.3 %reduce-scatter.33.cloned.1.call-start = ((), (), s32[]{:S(2)}) async-start(), calls=%async_computation.29 | async-start | bytes 1024000 | tf_op jit(solution)/shard_map/cond/branch_0_fun/reduce_scatter | solution.py:193
  472.7 21.8 %copy-start.15 = (bf16[80,1280]{1,0:T(8,128)(2,1)S(1)}, bf16[80,1280]{1,0:T(8,128)(2,1)}, u32[]{:S(2)}) copy-start(bf16[80,1280]{1,0:T(8,128)(2,1)} %reduce-scatter.23.cloned.1.call-done) | copy-start | bytes 614404 | tf_op jit(solution)/shard_map/cond
  478.4 36.4 %copy-start.13 = (bf16[320,1280]{1,0:T(8,128)(2,1)S(1)}, bf16[320,1280]{1,0:T(8,128)(2,1)}, u32[]{:S(2)}) copy-start(bf16[320,1280]{1,0:T(8,128)(2,1)} %copy-done.12) | copy-start | bytes 2457604 | tf_op jit(solution)/shard_map/cond
Sparse Core Ops, SparseCore 0:
  29.1 17.2 all-gather.46
  55.6 23.6 reduce-scatter.22
  105.1 25.9 reduce-scatter.24
  133.0 18.2 all-gather.18
  152.8 34.7 all-gather.16
  190.4 47.3 reduce-scatter.28
  240.8 47.9 reduce-scatter.26
  292.0 50.2 all-gather.20
  344.6 49.6 all-gather.22
  404.9 25.3 reduce-scatter.30
  431.8 18.2 all-gather.24
  472.9 21.6 reduce-scatter.32

commit v2 on v1

--- a/solution.py
+++ b/solution.py
@@ -96,6 +96,44 @@
     return jnp.dot(selection, values, preferred_element_type=jnp.float32)
 
 
+def shift_by(values, axis, step):
+    size = lax.axis_size(axis)
+    return lax.ppermute(values, axis, [(i, (i + step) % size) for i in range(size)])
+
+
+def sum_direct(part, axis):
+    total = part
+    for step in range(1, lax.axis_size(axis)):
+        total = total + shift_by(part, axis, step)
+    return total
+
+
+def gather_small(part, axis):
+    size = lax.axis_size(axis)
+    index = lax.axis_index(axis)
+    ids = jnp.arange(size, dtype=jnp.int32)[:, None]
+    out = jnp.where(ids == index, part[None, :], 0.0)
+    for step in range(1, size):
+        came = shift_by(part, axis, step)
+        out = jnp.where(ids == (index - step) % size, came[None, :], out)
+    return out.reshape(-1)
+
+
+def scatter_direct(partial, axis):
+    size = lax.axis_size(axis)
+    index = lax.axis_index(axis)
+    rows = partial.shape[0] // size
+
+    def piece(owner):
+        return lax.dynamic_slice_in_dim(partial, owner * rows, rows)
+
+    total = piece(index).astype(jnp.float32)
+    for step in range(1, size):
+        came = shift_by(piece((index + step) % size), axis, step)
+        total = total + came.astype(jnp.float32)
+    return total
+
+
 def packed_step(cap, sequence_in, operands):
     (
         merger_up,
@@ -111,17 +149,21 @@
     ) = operands
     n_row = lax.axis_size("row")
     n_col = lax.axis_size("col")
-    row_index = lax.axis_index("row")
     col_index = lax.axis_index("col")
     tokens = sequence_in.shape[0]
     held = hidden_cotangent.shape[0]
     packed = cap * n_col
-    rows_row = packed // n_row
     slot, rank, by_image, extra_slot = pack_plan(
         placement, patch_counts, tokens, n_row, n_col, cap
     )
     arrival = by_image.reshape(n_row, IMG_ROW, n_col, BLK // n_col)
-    arrival = jnp.transpose(arrival, (0, 2, 1, 3)).reshape(-1)
+    arrival = jnp.stack(
+        [
+            lax.dynamic_index_in_dim(arrival, (col_index - step) % n_col, axis=2, keepdims=False)
+            for step in range(n_col)
+        ],
+        axis=1,
+    ).reshape(-1)
     sequence = pick(one_hot(arrival, 0, packed), sequence_in).astype(jnp.bfloat16)
     slot_here = lax.dynamic_slice_in_dim(slot, col_index * held, held)
     cotangent = pick(one_hot(slot_here, col_index * cap, cap), hidden_cotangent)
@@ -139,50 +181,41 @@
     hidden_all = lax.all_gather(hidden_one, "col", axis=0, tiled=True)
     merged_out = lax.optimization_barrier(
         (
-            lax.psum_scatter(
-                pick(hidden_all, merger_down).astype(jnp.bfloat16),
-                "row",
-                scatter_dimension=0,
-                tiled=True,
-            ).astype(jnp.float32)
+            scatter_direct(pick(hidden_all, merger_down).astype(jnp.bfloat16), "row")
             + merger_down_bias.astype(jnp.float32)
         ).astype(jnp.bfloat16)
     )
 
     def row_sums(part):
-        spread = jnp.where(
-            jnp.arange(n_row, dtype=jnp.int32)[:, None] == row_index, part[None, :], 0.0
-        )
-        return lax.psum(spread.reshape(-1), ("row", "col"))
+        return gather_small(sum_direct(part, "col"), "row")
 
     merged_f = merged_out.astype(jnp.float32)
     merged_all = lax.all_gather(merged_out, "row", axis=0, tiled=True).astype(jnp.float32)
     square_sums = row_sums(jnp.sum(merged_f * merged_f, axis=1))
     inv_rms = lax.rsqrt(square_sums / D + EPS_NORM)
     gain = norm_gain.astype(jnp.float32)
-    normed_all = (merged_all * inv_rms[:, None] * gain).astype(jnp.bfloat16)
-
-    def gate_sums(weight):
+    normed_all = lax.optimization_barrier(
+        (merged_all * inv_rms[:, None] * gain).astype(jnp.bfloat16)
+    )
+
+    def block_sums(rows, weight):
         return lax.psum_scatter(
-            pick(normed_all, weight).astype(jnp.bfloat16), "col", scatter_dimension=0, tiled=True
+            pick(rows, weight).astype(jnp.bfloat16), "col", scatter_dimension=0, tiled=True
         )
 
-    gate_out = gate_sums(w_gate)
-    up_out = gate_sums(w_up)
+    gate_out = block_sums(normed_all, w_gate)
+    up_out = block_sums(normed_all, w_up)
     grad_gate, grad_up = swiglu_grads(gate_out, up_out, cotangent)
     grad_gate_all = lax.all_gather(grad_gate, "col", axis=0, tiled=True)
     grad_up_all = lax.all_gather(grad_up, "col", axis=0, tiled=True)
     from_gate = lax.dot_general(
         grad_gate_all, w_gate, CONTRACT_COLS, preferred_element_type=jnp.float32
     )
-    grad_normed = lax.psum_scatter(
-        (
-            from_gate
-            + lax.dot_general(grad_up_all, w_up, CONTRACT_COLS, preferred_element_type=jnp.float32)
-        ).astype(jnp.bfloat16),
-        "row",
-        scatter_dimension=0,
-        tiled=True,
+    from_up = lax.dot_general(
+        grad_up_all, w_up, CONTRACT_COLS, preferred_element_type=jnp.float32
+    )
+    grad_normed = scatter_direct((from_gate + from_up).astype(jnp.bfloat16), "row").astype(
+        jnp.bfloat16
     )
     inner = row_sums(jnp.sum(merged_f * (gain * grad_normed.astype(jnp.float32)), axis=1))
     gained_all = gain * lax.all_gather(grad_normed, "row", axis=0, tiled=True).astype(jnp.float32)
@@ -228,7 +261,10 @@
 ):
     n_col = lax.axis_size("col")
     held = hidden_cotangent.shape[0]
-    real_rows = lax.pmax(jnp.sum(patch_counts // 4), "group")
+    own_rows = jnp.sum(patch_counts // 4)
+    real_rows = own_rows
+    for step in range(1, lax.axis_size("group")):
+        real_rows = jnp.maximum(real_rows, shift_by(own_rows, "group", step))
     caps = [held * 5 // 8, held * 3 // 4, held]
     branch = sum((real_rows > cap * n_col).astype(jnp.int32) for cap in caps[:-1])
     image_tokens = patch_tokens(patches, patch_gain, patch_bias)
@@ -236,8 +272,14 @@
     feat_width = image_tokens.shape[2] // n_col
     sending = image_tokens.reshape(IMG_ROW * slot_count, n_col, feat_width)
     sending = jnp.transpose(sending, (1, 0, 2))
-    received = lax.all_to_all(sending, "col", split_axis=0, concat_axis=0, tiled=True)
-    merged = received.reshape(n_col * IMG_ROW * slot_count, feat_width)
+    col_index = lax.axis_index("col")
+    pieces = [lax.dynamic_index_in_dim(sending, col_index, keepdims=False)]
+    for step in range(1, n_col):
+        outgoing = lax.dynamic_index_in_dim(
+            sending, (col_index + step) % n_col, keepdims=False
+        )
+        pieces.append(shift_by(outgoing, "col", step))
+    merged = jnp.concatenate(pieces, axis=0)
     gathered_in = lax.all_gather(merged, "row", axis=0, tiled=True)
     operands = (
         merger_up,

time: 544 us -> 510 us (0.938)
  blocking collectives: 124 us -> 36.8 us
  starting transfers between devices: 0.83 us -> 27.4 us
  waiting for transfers between devices: 277 us -> 300 us
    psum x2 -> x0, blocking collectives: 65.7 us -> none  [row_sums(): return lax.psum(spread.reshape(-1), ('row', 'col'))]
    ppermute x0 -> x22, waiting for transfers between devices: none -> 47.8 us  [shift_by(): lax.ppermute(values, axis, [(i, (i + step) % size) for i in range(size)])]
    reduce_scatter x4 -> x2, waiting for transfers between devices: 135 us -> 97.4 us  [block_sums(): lax.psum_scatter(pick(rows, weight).astype(jnp.bfloat16), 'col', scatter_...]
    ppermute x0 -> x22, starting transfers between devices: none -> 26.8 us  [shift_by(): lax.ppermute(values, axis, [(i, (i + step) % size) for i in range(size)])]
    all_to_all x1 -> x0, blocking collectives: 16.5 us -> none  [shards(): lax.all_to_all(sending, 'col', split_axis=0, concat_axis=0, tiled=True)]
    all_gather x1, waiting for transfers between devices: 0.01 us -> 6.02 us  [packed_step(): lax.all_gather(grad_normed, 'row', axis=0, tiled=True).astype(jnp.float32)]
  transfers between devices with their start and end apart: 12 -> 32, of which waited for: 9 -> 29; matrix products, arithmetic and copies ran while one was open for 11% -> 11% of each run, Pallas kernels for 0% -> 0%
where the time goes in v2:
time: 510 us; the launch traced here: 502 us
  waiting for transfers between devices  300 us (59%)
  matrix products  86.8 us (17%)
  blocking collectives  36.8 us (7%)
  starting transfers between devices  27.4 us (5%)
  other arithmetic  20.2 us (4%)
  between operations  15.9 us (3%)
  loops' own time  9.62 us (2%)
  local copies, waits for them, and re-layouts  5.29 us (1%)
    reduce_scatter x2, waiting for transfers between devices, block_sums(): lax.psum_scatter(pick(rows, weight).astype(jnp.bfloat16), 'col', scatter_...  97.4 us
    dot_general x8, matrix products, pick(): return jnp.dot(selection, values, preferred_element_type=jnp.float32)  51.3 us
    all_gather x1, waiting for transfers between devices, packed_step(): grad_gate_all = lax.all_gather(grad_gate, 'col', axis=0, tiled=True)  49.4 us
    ppermute x22, waiting for transfers between devices, shift_by(): lax.ppermute(values, axis, [(i, (i + step) % size) for i in range(size)])  47.8 us
    all_gather x1, waiting for transfers between devices, packed_step(): grad_up_all = lax.all_gather(grad_up, 'col', axis=0, tiled=True)  41.5 us
    ppermute x22, starting transfers between devices, shift_by(): lax.ppermute(values, axis, [(i, (i + step) % size) for i in range(size)])  26.8 us
    reduce_scatter x1, waiting for transfers between devices, packed_step(): lax.psum_scatter(pick(sequence, merger_up).astype(jnp.bfloat16), 'col', s...  23.7 us
    all_gather x1, blocking collectives, packed_step(): grad_pre_all = lax.all_gather(grad_pre, 'col', axis=0, tiled=True)  18.4 us
  transfers between devices with their start and end apart: 32, of which 29 were waited for; matrix products, arithmetic and copies ran while one was open for 11% of the time, Pallas kernels for 0%

profile of v2, /device:TPU:0, one launch (start us, length us, event | category | flops | bytes accessed | tf_op | source)
XLA Modules:
  0.0 502.4 jit_solution(12320023446325932657)
XLA Ops:
  7.3 1.1 convert_reduce_fusion.6
  8.4 1.2 fusion.134
  11.1 1.2 fusion.137
  13.1 5.1 %collective-permute-start.57 = (bf16[32,1280]{1,0:T(8,128)(2,1)S(1)}, bf16[32,1280]{1,0:T(8,128)(2,1)S(1)}, u32[]{:S(2)}, u32[]{:S(2)}) collective-permute-start(bf16[32,1280]{1,0:T(8,128)(2,1)S(1)} %bitcast.131), channel_id=1, source_target_pairs={{0,3},{1,0},{2,1},{3,2},{4,7},{5,4},{6,5},{7,6},{8,11},{9,8},{10,9... | collective-permute-start | bytes 245768 | tf_op jit(solution)/shard_map/ppermute | solution.py:101
  18.3 1.1 collective-permute-start.56
  19.4 1.7 collective-permute-done.57
  21.1 3.9 collective-permute-done.55
  25.0 1.7 collective-permute-done.56
  28.1 1.5 collective-permute-start.54
  29.7 2.3 collective-permute-done.54
  33.1 12.2 %all-gather.47.cloned.1.call-done = bf16[512,1280]{1,0:T(8,128)(2,1)} async-done(((bf16[128,1280]{1,0:T(8,128)(2,1)}), bf16[512,1280]{1,0:T(8,128)(2,1)}) %all-gather.47.cloned.1.call-update) | async-done | bytes 1310736 | tf_op jit(solution)/shard_map/all_gather | solution.py:283
  45.4 449.7 %conditional.1 = (f32[1280,1280]{1,0:T(8,128)}, f32[1280]{0:T(1024)}, f32[1280,2048]{1,0:T(8,128)}, f32[2048]{0:T(1024)}) conditional(s32[]{:T(128)} %clamp.3, (s32[32]{0:T(128)S(1)}, s32[32]{0:T(128)S(1)}, bf16[512,1280]{1,0:T(8,128)(2,1)}, bf16[1280,1280]{1,0:T(8,128)(2,1)}, bf16[1280]{0:T(1024)(128)(2,1)S(1)}, ...), branch_computations={%region_3.21_spmd, %region_21.39_spmd, %region_39.56_spmd} | conditional | flops 43256897536 | bytes 340842208 | solution.py:296
  47.7 1.9 convolution_convert_fusion.3
  50.5 4.1 convolution_convert_fusion.6
  54.7 23.7 %reduce-scatter.17.cloned.1.call-done = bf16[80,1280]{1,0:T(8,128)(2,1)} async-done(((bf16[320,1280]{1,0:T(8,128)(2,1)}), bf16[80,1280]{1,0:T(8,128)(2,1)}) %reduce-scatter.17.cloned.1.call-update) | async-done | bytes 204816 | tf_op jit(solution)/shard_map/cond/branch_0_fun/reduce_scatter | solution.py:177
  78.4 1.8 fusion.19
  80.2 18.4 %all_gather.42 = bf16[320,1280]{1,0:T(8,128)(2,1)S(1)} all-gather(bf16[80,1280]{1,0:T(8,128)(2,1)S(1)} %fusion.19), channel_id=1, replica_groups=mesh['group'=2,'row'=4,'col'=4] {'col'}, dimensions={0}, use_global_device_ids=true | all-gather | bytes 1024000 | tf_op jit(solution)/shard_map/cond/branch_0_fun/all_gather | solution.py:181
  98.6 4.4 convolution_convert_fusion.5
  103.0 1.0 constant_dynamic-slice_fusion.3
  104.0 1.7 collective-permute-start.2
  105.8 1.5 collective-permute-start.1
  107.2 5.1 %collective-permute-done = bf16[80,2048]{1,0:T(8,128)(2,1)S(1)} collective-permute-done((bf16[80,2048]{1,0:T(8,128)(2,1)}, bf16[80,2048]{1,0:T(8,128)(2,1)S(1)}, u32[]{:S(2)}, u32[]{:S(2)}) %collective-permute-start) | collective-permute-done | bytes 327712 | tf_op jit(solution)/shard_map/cond/branch_0_fun/ppermute | solution.py:101
  112.4 1.8 collective-permute-done.2
  114.1 7.2 %collective-permute-done.1 = bf16[80,2048]{1,0:T(8,128)(2,1)} collective-permute-done((bf16[80,2048]{1,0:T(8,128)(2,1)}, bf16[80,2048]{1,0:T(8,128)(2,1)}, u32[]{:S(2)}, u32[]{:S(2)}) %collective-permute-start.1) | collective-permute-done | bytes 327712 | tf_op jit(solution)/shard_map/cond/branch_0_fun/ppermute | solution.py:101
  121.4 2.0 add_convert_fusion.1
  124.2 1.2 convolution_convert_fusion.2
  125.8 1.9 collective-permute-start.5
  127.7 1.0 collective-permute-start.3
  129.3 2.8 collective-permute-done.4
  133.0 1.6 collective-permute-start.7
  134.6 1.9 collective-permute-start.6
  136.6 1.1 collective-permute-done.6
  137.9 3.3 all-gather.19.cloned.1.call-done
  141.2 1.7 fusion.4
  142.9 1.1 copy-done.10
  144.0 16.6 %convolution_convert_fusion = bf16[320,3696]{1,0:T(8,128)(2,1)} fusion(bf16[320,2048]{1,0:T(8,128)(2,1)S(1)} %fusion.4, bf16[2048,3696]{0,1:T(8,128)(2,1)} %get-tuple-element.216), kind=kOutput, calls=%fused_computation | convolution fusion | flops 4845603840 | bytes 18814976 | tf_op jit(solution)/shard_map/cond/branch_0_fun/dot_general | solution.py:96
  160.7 16.9 %convolution_convert_fusion.1 = bf16[320,3696]{1,0:T(8,128)(2,1)} fusion(bf16[320,2048]{1,0:T(8,128)(2,1)} %copy-done.10, bf16[2048,3696]{0,1:T(8,128)(2,1)} %get-tuple-element.215), kind=kOutput, calls=%fused_computation.1 | convolution fusion | flops 4845603840 | bytes 18814976 | tf_op jit(solution)/shard_map/cond/branch_0_fun/dot_general | solution.py:96
  178.1 2.7 fusion.37
  180.8 46.7 %reduce-scatter.21.cloned.1.call-done = bf16[80,3696]{1,0:T(8,128)(2,1)} async-done(((bf16[320,3696]{1,0:T(8,128)(2,1)}), bf16[80,3696]{1,0:T(8,128)(2,1)}) %reduce-scatter.21.cloned.1.call-update) | async-done | bytes 591376 | tf_op jit(solution)/shard_map/cond/branch_0_fun/reduce_scatter | solution.py:202
  227.5 50.7 %reduce-scatter.19.cloned.1.call-done = bf16[80,3696]{1,0:T(8,128)(2,1)} async-done(((bf16[320,3696]{1,0:T(8,128)(2,1)}), bf16[80,3696]{1,0:T(8,128)(2,1)}) %reduce-scatter.19.cloned.1.call-update) | async-done | bytes 591376 | tf_op jit(solution)/shard_map/cond/branch_0_fun/reduce_scatter | solution.py:202
  278.2 3.4 fusion.14
  282.6 49.4 %all-gather.21.cloned.1.call-done = bf16[320,3696]{1,0:T(8,128)(2,1)} async-done(((bf16[80,3696]{1,0:T(8,128)(2,1)}), bf16[320,3696]{1,0:T(8,128)(2,1)}) %all-gather.21.cloned.1.call-update) | async-done | bytes 2365456 | tf_op jit(solution)/shard_map/cond/branch_0_fun/all_gather | solution.py:209
  332.1 10.3 %fusion.142 = f32[320,2048]{1,0:T(8,128)} fusion(bf16[320,3696]{1,0:T(8,128)(2,1)} %all-gather.21.cloned.1.call-done, bf16[2048,3696]{0,1:T(8,128)(2,1)} %get-tuple-element.216), kind=kOutput, calls=%fused_computation.430 | convolution fusion | flops 4844421120 | bytes 20125696 | tf_op jit(solution)/shard_map/cond/branch_0_fun/dot_general | solution.py:211
  342.4 41.5 %all-gather.23.cloned.1.call-done = bf16[320,3696]{1,0:T(8,128)(2,1)} async-done(((bf16[80,3696]{1,0:T(8,128)(2,1)}), bf16[320,3696]{1,0:T(8,128)(2,1)}) %all-gather.23.cloned.1.call-update) | async-done | bytes 2365456 | tf_op jit(solution)/shard_map/cond/branch_0_fun/all_gather | solution.py:210
  383.8 9.7 %fusion.2 = bf16[320,2048]{1,0:T(8,128)(2,1)S(1)} fusion(f32[320,2048]{1,0:T(8,128)} %fusion.142, bf16[320,3696]{1,0:T(8,128)(2,1)} %all-gather.23.cloned.1.call-done, bf16[2048,3696]{0,1:T(8,128)(2,1)} %get-tuple-element.215), kind=kOutput, calls=%fused_computation.10 | convolution fusion | flops 4845731840 | bytes 21436416 | tf_op jit(solution)/shard_map/cond/branch_0_fun/dot_general | solution.py:214
  393.6 1.7 collective-permute-start.11
  395.4 1.5 collective-permute-start.10
  396.8 5.0 collective-permute-done.9
  401.8 1.6 collective-permute-done.11
  403.4 7.2 %collective-permute-done.10 = bf16[80,2048]{1,0:T(8,128)(2,1)S(1)} collective-permute-done((bf16[80,2048]{1,0:T(8,128)(2,1)S(1)}, bf16[80,2048]{1,0:T(8,128)(2,1)S(1)}, u32[]{:S(2)}, u32[]{:S(2)}) %collective-permute-start.10) | collective-permute-done | bytes 327712 | tf_op jit(solution)/shard_map/cond/branch_0_fun/ppermute | solution.py:101
  410.7 1.1 fusion.16
  413.2 1.9 collective-permute-start.12
  415.4 1.8 collective-permute-done.13
  417.2 1.4 collective-permute-done.12
  418.6 1.6 collective-permute-start.16
  420.1 1.4 collective-permute-start.15
  423.0 6.0 %all-gather.25.cloned.1.call-done = bf16[320,2048]{1,0:T(8,128)(2,1)} async-done(((bf16[80,2048]{1,0:T(8,128)(2,1)}), bf16[320,2048]{1,0:T(8,128)(2,1)}) %all-gather.25.cloned.1.call-update) | async-done | bytes 1310736 | tf_op jit(solution)/shard_map/cond/branch_0_fun/all_gather | solution.py:221
  429.0 3.0 convert_reduce_fusion
  432.0 5.3 %convolution_convert_fusion.4 = bf16[320,1280]{1,0:T(8,128)(2,1)} fusion(bf16[320,2048]{1,0:T(8,128)(2,1)S(1)} %get-tuple-element.240, bf16[1280,2048]{1,0:T(8,128)(2,1)} %get-tuple-element.71), kind=kOutput, calls=%fused_computation.11 | convolution fusion | flops 1678131200 | bytes 7372800 | tf_op jit(solution)/shard_map/cond/branch_0_fun/dot_general | solution.py:227
  437.3 5.7 %fusion.144 = f32[1280,2048]{1,0:T(8,128)} fusion(bf16[320,1280]{1,0:T(8,128)(2,1)S(1)} %all_gather.42, bf16[320,2048]{1,0:T(8,128)(2,1)S(1)} %get-tuple-element.240), kind=kOutput, calls=%fused_computation.432 | convolution fusion | flops 1677721600 | bytes 12615680 | tf_op jit(solution)/shard_map/cond/branch_0_fun/dot_general | solution.py:234
  443.0 18.1 %reduce-scatter.23.cloned.1.call-done = bf16[80,1280]{1,0:T(8,128)(2,1)} async-done(((bf16[320,1280]{1,0:T(8,128)(2,1)}), bf16[80,1280]{1,0:T(8,128)(2,1)}) %reduce-scatter.23.cloned.1.call-update) | async-done | bytes 204816 | tf_op jit(solution)/shard_map/cond/branch_0_fun/reduce_scatter | solution.py:226
  461.1 1.1 fusion.25
  462.3 18.4 %all_gather.48 = bf16[320,1280]{1,0:T(8,128)(2,1)S(1)} all-gather(bf16[80,1280]{1,0:T(8,128)(2,1)S(1)} %fusion.25), channel_id=1, replica_groups=mesh['group'=2,'row'=4,'col'=4] {'col'}, dimensions={0}, use_global_device_ids=true | all-gather | bytes 1024000 | tf_op jit(solution)/shard_map/cond/branch_0_fun/all_gather | solution.py:239
  481.4 4.7 fusion.143
  (126 shorter events, 15.4 us)
Async XLA Ops:
  7.2 38.2 %all-gather.47.cloned.1.call-start = ((), (), s32[]{:S(2)}) async-start(), calls=%async_computation.39 | async-start | bytes 1638400 | tf_op jit(solution)/shard_map/all_gather | solution.py:283
  9.5 18.0 %copy-start.38 = (s32[32]{0:T(128)S(1)}, s32[32]{0:T(128)}, u32[]{:S(2)}) copy-start(s32[32]{0:T(128)} %param.28) | copy-start | bytes 388
  9.6 35.8 %copy-start = (bf16[128,3696]{0,1:T(8,128)(2,1)S(1)}, bf16[128,3696]{0,1:T(8,128)(2,1)}, u32[]{:S(2)}) copy-start(bf16[128,3696]{0,1:T(8,128)(2,1)} %param.26) | copy-start | bytes 2838532
  9.6 35.8 %copy-start.15 = (bf16[1280]{0:T(1024)(128)(2,1)S(1)}, bf16[1280]{0:T(1024)(128)(2,1)}, u32[]{:S(2)}) copy-start(bf16[1280]{0:T(1024)(128)(2,1)} %param.20) | copy-start | bytes 7684
  9.6 35.8 %copy-start.16 = (bf16[2048]{0:T(1024)(128)(2,1)S(1)}, bf16[2048]{0:T(1024)(128)(2,1)}, u32[]{:S(2)}) copy-start(bf16[2048]{0:T(1024)(128)(2,1)} %param.22) | copy-start | bytes 12292
  9.6 35.8 %copy-start.17 = (bf16[2048]{0:T(1024)(128)(2,1)S(1)}, bf16[2048]{0:T(1024)(128)(2,1)}, u32[]{:S(2)}) copy-start(bf16[2048]{0:T(1024)(128)(2,1)} %param.23) | copy-start | bytes 12292
  9.6 35.8 %copy-start.18 = (s32[32]{0:T(128)S(1)}, s32[32]{0:T(128)}, u32[]{:S(2)}) copy-start(s32[32]{0:T(128)} %param.27) | copy-start | bytes 388
  13.1 8.0 %collective-permute-start.57 = (bf16[32,1280]{1,0:T(8,128)(2,1)S(1)}, bf16[32,1280]{1,0:T(8,128)(2,1)S(1)}, u32[]{:S(2)}, u32[]{:S(2)}) collective-permute-start(bf16[32,1280]{1,0:T(8,128)(2,1)S(1)} %bitcast.131), channel_id=1, source_target_pairs={{0,3},{1,0},{2,1},{3,2},{4,7},{5,4},{6,5},{7,6},{8,11},{9,8},{10,9... | collective-permute-start | bytes 245768 | tf_op jit(solution)/shard_map/ppermute | solution.py:101
  18.3 6.7 %collective-permute-start.55 = (bf16[32,1280]{1,0:T(8,128)(2,1)S(1)}, bf16[32,1280]{1,0:T(8,128)(2,1)S(1)}, u32[]{:S(2)}, u32[]{:S(2)}) collective-permute-start(bf16[32,1280]{1,0:T(8,128)(2,1)S(1)} %bitcast.132), channel_id=1, source_target_pairs={{0,1},{1,2},{2,3},{3,0},{4,5},{5,6},{6,7},{7,4},{8,9},{9,10},{10,1... | collective-permute-start | bytes 245768 | tf_op jit(solution)/shard_map/ppermute | solution.py:101
  18.3 8.4 %collective-permute-start.56 = (bf16[32,1280]{1,0:T(8,128)(2,1)S(1)}, bf16[32,1280]{1,0:T(8,128)(2,1)S(1)}, u32[]{:S(2)}, u32[]{:S(2)}) collective-permute-start(bf16[32,1280]{1,0:T(8,128)(2,1)S(1)} %bitcast.133), channel_id=1, source_target_pairs={{0,2},{1,3},{2,0},{3,1},{4,6},{5,7},{6,4},{7,5},{8,10},{9,11},{10,... | collective-permute-start | bytes 245768 | tf_op jit(solution)/shard_map/ppermute | solution.py:101
  28.1 3.8 collective-permute-start.54
  45.4 33.0 %reduce-scatter.17.cloned.1.call-start = ((), (), s32[]{:S(2)}) async-start(), calls=%async_computation.12 | async-start | bytes 1024000 | tf_op jit(solution)/shard_map/cond/branch_0_fun/reduce_scatter | solution.py:177
  49.6 0.9 copy-start.11
  54.6 86.6 %all-gather.19.cloned.1.call-start = ((), (), s32[]{:S(2)}) async-start(), calls=%async_computation.14 | async-start | bytes 1638400 | tf_op jit(solution)/shard_map/cond/branch_0_fun/all_gather | solution.py:193
  104.0 8.4 %collective-permute-start = (bf16[80,2048]{1,0:T(8,128)(2,1)}, bf16[80,2048]{1,0:T(8,128)(2,1)S(1)}, u32[]{:S(2)}, u32[]{:S(2)}) collective-permute-start(bf16[80,2048]{1,0:T(8,128)(2,1)} %get-tuple-element.256), channel_id=1, source_target_pairs={{0,4},{4,8},{8,12},{12,0},{1,5},{5,9},{9,13},{13,1},{2,6},{6,10},{... | collective-permute-start | bytes 983048 | tf_op jit(solution)/shard_map/cond/branch_0_fun/ppermute | solution.py:101
  104.0 10.1 %collective-permute-start.2 = (bf16[80,2048]{1,0:T(8,128)(2,1)}, bf16[80,2048]{1,0:T(8,128)(2,1)}, u32[]{:S(2)}, u32[]{:S(2)}) collective-permute-start(bf16[80,2048]{1,0:T(8,128)(2,1)} %get-tuple-element.257), channel_id=1, source_target_pairs={{0,12},{4,0},{8,4},{12,8},{1,13},{5,1},{9,5},{13,9},{2,14},{6,2},{... | collective-permute-start | bytes 983048 | tf_op jit(solution)/shard_map/cond/branch_0_fun/ppermute | solution.py:101
  105.8 15.6 %collective-permute-start.1 = (bf16[80,2048]{1,0:T(8,128)(2,1)}, bf16[80,2048]{1,0:T(8,128)(2,1)}, u32[]{:S(2)}, u32[]{:S(2)}) collective-permute-start(bf16[80,2048]{1,0:T(8,128)(2,1)} %get-tuple-element.258), channel_id=1, source_target_pairs={{0,8},{4,12},{8,0},{12,4},{1,9},{5,13},{9,1},{13,5},{2,10},{6,14},... | collective-permute-start | bytes 983048 | tf_op jit(solution)/shard_map/cond/branch_0_fun/ppermute | solution.py:101
  123.4 2.2 copy-start.4
  123.4 54.7 %all-gather.17.cloned.1.call-start = ((), (), s32[]{:S(2)}) async-start(), calls=%async_computation.13 | async-start | bytes 1781760 | tf_op jit(solution)/shard_map/cond/branch_0_fun/all_gather | solution.py:173
  125.5 102.0 %reduce-scatter.21.cloned.1.call-start = ((), (), s32[]{:S(2)}) async-start(), calls=%async_computation.16 | async-start | bytes 2969600 | tf_op jit(solution)/shard_map/cond/branch_0_fun/reduce_scatter | solution.py:202
  125.8 3.6 collective-permute-start.5
  127.7 4.4 collective-permute-start.4
  127.7 5.3 %collective-permute-start.3 = (f32[80]{0:T(128)S(1)}, f32[80]{0:T(128)S(1)}, u32[]{:S(2)}, u32[]{:S(2)}) collective-permute-start(f32[80]{0:T(128)S(1)} %fusion.15), channel_id=1, source_target_pairs={{0,1},{1,2},{2,3},{3,0},{4,5},{5,6},{6,7},{7,4},{8,9},{9,10},{10,1... | collective-permute-start | bytes 968 | tf_op jit(solution)/shard_map/cond/branch_0_fun/ppermute | solution.py:101
  133.0 3.5 collective-permute-start.8
  133.0 3.6 collective-permute-start.7
  134.6 3.2 collective-permute-start.6
  142.9 1.1 copy-start.10
  160.7 117.6 %reduce-scatter.19.cloned.1.call-start = ((), (), s32[]{:S(2)}) async-start(), calls=%async_computation.15 | async-start | bytes 2969600 | tf_op jit(solution)/shard_map/cond/branch_0_fun/reduce_scatter | solution.py:202
  177.6 154.4 %all-gather.21.cloned.1.call-start = ((), (), s32[]{:S(2)}) async-start(), calls=%async_computation.17 | async-start | bytes 2969600 | tf_op jit(solution)/shard_map/cond/branch_0_fun/all_gather | solution.py:209
  281.7 102.2 %all-gather.23.cloned.1.call-start = ((), (), s32[]{:S(2)}) async-start(), calls=%async_computation.18 | async-start | bytes 2969600 | tf_op jit(solution)/shard_map/cond/branch_0_fun/all_gather | solution.py:210
  282.4 146.6 %all-gather.25.cloned.1.call-start = ((), (), s32[]{:S(2)}) async-start(), calls=%async_computation.19 | async-start | bytes 1638400 | tf_op jit(solution)/shard_map/cond/branch_0_fun/all_gather | solution.py:221
  393.6 8.2 %collective-permute-start.9 = (bf16[80,2048]{1,0:T(8,128)(2,1)S(1)}, bf16[80,2048]{1,0:T(8,128)(2,1)S(1)}, u32[]{:S(2)}, u32[]{:S(2)}) collective-permute-start(bf16[80,2048]{1,0:T(8,128)(2,1)S(1)} %get-tuple-element.253), channel_id=1, source_target_pairs={{0,4},{4,8},{8,12},{12,0},{1,5},{5,9},{9,13},{13,1},{2,6},{6,10},{... | collective-permute-start | bytes 983048 | tf_op jit(solution)/shard_map/cond/branch_0_fun/ppermute | solution.py:101
  393.6 9.8 %collective-permute-start.11 = (bf16[80,2048]{1,0:T(8,128)(2,1)S(1)}, bf16[80,2048]{1,0:T(8,128)(2,1)S(1)}, u32[]{:S(2)}, u32[]{:S(2)}) collective-permute-start(bf16[80,2048]{1,0:T(8,128)(2,1)S(1)} %get-tuple-element.254), channel_id=1, source_target_pairs={{0,12},{4,0},{8,4},{12,8},{1,13},{5,1},{9,5},{13,9},{2,14},{6,2},{... | collective-permute-start | bytes 983048 | tf_op jit(solution)/shard_map/cond/branch_0_fun/ppermute | solution.py:101
  395.4 15.3 %collective-permute-start.10 = (bf16[80,2048]{1,0:T(8,128)(2,1)S(1)}, bf16[80,2048]{1,0:T(8,128)(2,1)S(1)}, u32[]{:S(2)}, u32[]{:S(2)}) collective-permute-start(bf16[80,2048]{1,0:T(8,128)(2,1)S(1)} %get-tuple-element.255), channel_id=1, source_target_pairs={{0,8},{4,12},{8,0},{12,4},{1,9},{5,13},{9,1},{13,5},{2,10},{6,14},... | collective-permute-start | bytes 983048 | tf_op jit(solution)/shard_map/cond/branch_0_fun/ppermute | solution.py:101
  411.8 49.3 %reduce-scatter.23.cloned.1.call-start = ((), (), s32[]{:S(2)}) async-start(), calls=%async_computation.20 | async-start | bytes 1024000 | tf_op jit(solution)/shard_map/cond/branch_0_fun/reduce_scatter | solution.py:226
  411.8 3.6 collective-permute-start.14
  412.8 4.4 collective-permute-start.13
  413.2 5.3 %collective-permute-start.12 = (f32[80]{0:T(128)S(1)}, f32[80]{0:T(128)S(1)}, u32[]{:S(2)}, u32[]{:S(2)}) collective-permute-start(f32[80]{0:T(128)S(1)} %get-tuple-element.241), channel_id=1, source_target_pairs={{0,1},{1,2},{2,3},{3,0},{4,5},{5,6},{6,7},{7,4},{8,9},{9,10},{10,1... | collective-permute-start | bytes 968 | tf_op jit(solution)/shard_map/cond/branch_0_fun/ppermute | solution.py:101
  418.6 3.0 collective-permute-start.17
  418.6 3.6 collective-permute-start.16
  420.1 2.7 collective-permute-start.15
  437.3 23.8 %copy-start.14 = (bf16[80,1280]{1,0:T(8,128)(2,1)S(1)}, bf16[80,1280]{1,0:T(8,128)(2,1)}, u32[]{:S(2)}) copy-start(bf16[80,1280]{1,0:T(8,128)(2,1)} %reduce-scatter.17.cloned.1.call-done) | copy-start | bytes 614404 | tf_op jit(solution)/shard_map/cond
  443.0 38.4 %copy-start.12 = (bf16[320,1280]{1,0:T(8,128)(2,1)S(1)}, bf16[320,1280]{1,0:T(8,128)(2,1)}, u32[]{:S(2)}) copy-start(bf16[320,1280]{1,0:T(8,128)(2,1)} %copy-done.11) | copy-start | bytes 2457604 | tf_op jit(solution)/shard_map/cond
Sparse Core Ops, SparseCore 0:
  27.6 17.7 all-gather.46
  54.7 23.6 reduce-scatter.16
  123.5 17.6 all-gather.18
  142.7 34.6 all-gather.16
  180.1 47.3 reduce-scatter.20
  230.2 47.9 reduce-scatter.18
  281.8 50.2 all-gather.20
  334.2 49.5 all-gather.22
  411.9 17.0 all-gather.24
  437.4 23.6 reduce-scatter.22
